TPU v7x, 32 devices: a whole 2x2x4 slice. The times are simulated.
32 devices in a mesh: inter: 16 (over z, y, x), intra: 2 (over core).
Axes of the slice: x: 2, y: 2, z: 4, core: 2. Of those that a mesh axis runs over, the one named last changes fastest.
Arguments:
- tokens: bfloat16 [2048, 4096], P('inter', 'intra'), may hold values from -6 to 6
- gate_codes: bfloat16 [7168, 4096], P(('intra', 'inter')), may hold values from -127 to 127
- gate_scales: float32 [7168, 16], P(('intra', 'inter')), may hold values from 0.0001 to 0.0005
- up_codes: bfloat16 [7168, 4096], P(('intra', 'inter')), may hold values from -127 to 127
- up_scales: float32 [7168, 16], P(('intra', 'inter')), may hold values from 0.0001 to 0.0005
- cotangent: bfloat16 [2048, 7168], P('inter', 'intra'), may hold values from -6 to 6
Outputs:
- hidden: bfloat16 [2048, 7168], P('inter', 'intra')
- token_grad: bfloat16 [2048, 4096], P('inter', 'intra')
- gate_grad: float32 [7168, 4096], P(('intra', 'inter'))
- up_grad: float32 [7168, 4096], P(('intra', 'inter'))
All inputs are finite; a program needn't handle non-finite values.
Results may differ from a plain program's by a relative error of at most 0.02.
Values may be sent and summed in bfloat16 or wider, within the bound.
A program may use at most 384 MiB of HBM per device.

v0:
```python
import jax
import jax.numpy as jnp
from jax import lax
from jax.sharding import PartitionSpec as P


def dequantize(codes, scales):
    rows, width = codes.shape
    blocks = scales.shape[1]
    values = codes.astype(jnp.float32).reshape(rows, blocks, width // blocks) * scales[:, :, None]
    return values.reshape(rows, width).astype(jnp.bfloat16)


def per_device(tokens, gate_codes, gate_scales, up_codes, up_scales, cotangent):
    whole = lax.all_gather(tokens, "intra", axis=1, tiled=True)
    codes_gate, scales_gate = (
        lax.all_gather(gate_codes, "inter", axis=0, tiled=True),
        lax.all_gather(gate_scales.astype(jnp.bfloat16), "inter", axis=0, tiled=True).astype(
            gate_scales.dtype
        ),
    )
    codes_up, scales_up = (
        lax.all_gather(up_codes, "inter", axis=0, tiled=True),
        lax.all_gather(up_scales.astype(jnp.bfloat16), "inter", axis=0, tiled=True).astype(
            up_scales.dtype
        ),
    )
    w_gate = dequantize(codes_gate, scales_gate)
    w_up = dequantize(codes_up, scales_up)
    gate = jnp.einsum("td,fd->tf", whole, w_gate, preferred_element_type=jnp.float32)
    up = jnp.einsum("td,fd->tf", whole, w_up, preferred_element_type=jnp.float32)
    sig = jax.nn.sigmoid(gate)
    act = gate * sig
    hidden = (act * up).astype(jnp.bfloat16)
    back = cotangent.astype(jnp.float32)
    d_up = (back * act).astype(jnp.bfloat16)
    d_gate = (back * up * sig * (1.0 + gate * (1.0 - sig))).astype(jnp.bfloat16)
    groups = lax.axis_size("inter")
    owned = gate_codes.shape[0]

    def blocked(term):
        return term.astype(jnp.bfloat16).reshape(groups, owned, term.shape[1])

    partial_sum = jnp.dot(d_gate, w_gate, preferred_element_type=jnp.float32)
    partial_sum = partial_sum + jnp.dot(d_up, w_up, preferred_element_type=jnp.float32)
    token_grad = lax.psum_scatter(
        partial_sum.astype(jnp.bfloat16), "intra", scatter_dimension=1, tiled=True
    )
    gate_rows_in = lax.all_to_all(
        blocked(jnp.einsum("tf,td->fd", d_gate, whole, preferred_element_type=jnp.float32)),
        "inter",
        split_axis=0,
        concat_axis=0,
        tiled=True,
    )
    up_rows_in = lax.all_to_all(
        blocked(jnp.einsum("tf,td->fd", d_up, whole, preferred_element_type=jnp.float32)),
        "inter",
        split_axis=0,
        concat_axis=0,
        tiled=True,
    )
    gate_part = jnp.sum(gate_rows_in.astype(jnp.float32), axis=0)
    up_part = jnp.sum(up_rows_in.astype(jnp.float32), axis=0)
    gate_grad = gate_part / groups
    up_grad = up_part / groups
    return (hidden, token_grad, gate_grad, up_grad)


def solution(mesh):
    return jax.shard_map(
        per_device,
        mesh=mesh,
        in_specs=(
            P("inter", "intra"),
            P(("intra", "inter"), None),
            P(("intra", "inter"), None),
            P(("intra", "inter"), None),
            P(("intra", "inter"), None),
            P("inter", "intra"),
        ),
        out_specs=(
            P("inter", "intra"),
            P("inter", "intra"),
            P(("intra", "inter"), None),
            P(("intra", "inter"), None),
        ),
        check_vma=False,
    )
```

profile of v0, /device:TPU:28, one launch (start us, length us, event | category | flops | bytes accessed | tf_op | source)
XLA Modules:
  0.0 2071.9 jit_solution(7090375887927481468)
XLA Ops:
  7.2 0.0 copy-start.2
  7.2 0.0 all-gather.8.cloned.1.call-start
  7.2 0.7 all-gather.8.cloned.1.call-update
  7.9 0.0 all-gather.6.cloned.1.call-start
  8.0 0.7 all-gather.6.cloned.1.call-update
  8.7 0.0 all-gather.10.cloned.1.call-start
  8.7 0.7 all-gather.10.cloned.1.call-update
  9.4 0.0 copy-done.2
  9.4 36.1 %all-gather = bf16[16,224,16]{1,2,0:T(8,128)(2,1)S(1)} all-gather(bf16[1,224,16]{1,2,0:T(8,128)(2,1)S(1)} %convert_bitcast_fusion.1), channel_id=1, replica_groups=mesh['inter'=16,'intra'=2] {'inter'}, dimensions={0}, use_global_device_ids=true | all-gather | bytes 121856 | tf_op jit(solution)/shard_map/all_gather | solution.py:18
  45.5 0.3 copy.24
  45.8 19.1 mul.43
  64.9 0.0 copy-start.1
  64.9 0.0 copy-start.3
  64.9 64.6 %copy.28 = f32[448,8,16,256]{3,1,2,0:T(8,128)} copy(f32[448,8,16,256]{3,2,1,0:T(8,128)} %bitcast.26) | data formatting | bytes 117440512
  129.5 0.0 copy-done.1
  129.5 0.6 copy.22
  130.1 0.0 copy-done.3
  130.1 40.0 %all-gather.1 = bf16[16,224,16]{1,2,0:T(8,128)(2,1)S(1)} all-gather(bf16[1,224,16]{1,2,0:T(8,128)(2,1)S(1)} %convert_bitcast_fusion), channel_id=1, replica_groups=mesh['inter'=16,'intra'=2] {'inter'}, dimensions={0}, use_global_device_ids=true | all-gather | bytes 121856 | tf_op jit(solution)/shard_map/all_gather | solution.py:24
  170.1 0.3 copy.25
  170.5 22.7 %mul.47 = f32[3584,16,256]{2,1,0:T(8,128)} broadcast(f32[3584,16]{1,0:T(8,128)S(1)} %bitcast.31), dimensions={0,1} | broadcast | bytes 58949632 | tf_op jit(solution)/shard_map/mul | solution.py:10
  193.2 64.5 %copy.29 = f32[448,8,16,256]{3,1,2,0:T(8,128)} copy(f32[448,8,16,256]{3,2,1,0:T(8,128)} %bitcast.27) | data formatting | bytes 117440512
  257.7 0.0 all-gather.8.cloned.1.call-done
  257.7 76.2 %all-gather.6.cloned.1.call-done = bf16[3584,4096]{1,0:T(8,128)(2,1)} async-done(((bf16[224,4096]{1,0:T(8,128)(2,1)}), bf16[3584,4096]{1,0:T(8,128)(2,1)}) %all-gather.6.cloned.1.call-update) | async-done | bytes 29360144 | tf_op jit(solution)/shard_map/all_gather | solution.py:17
  333.8 30.7 %convolution_bitcast_fusion.1 = f32[128,3584]{0,1:T(8,128)S(1)} fusion(bf16[128,4096]{1,0:T(8,128)(2,1)} %all-gather.8.cloned.1.call-done, f32[3584,4096]{1,0:T(8,128)} %bitcast.22, bf16[3584,4096]{1,0:T(8,128)(2,1)} %all-gather.6.cloned.1.call-done), kind=kOutput, calls=%fused_computation.7 | convolution fusion | flops 3802136576 | bytes 90963968 | tf_op jit(solution)/shard_map/td,fd->tf/dot_general | solution.py:30
  364.5 280.5 %all-gather.10.cloned.1.call-done = bf16[3584,4096]{1,0:T(8,128)(2,1)} async-done(((bf16[224,4096]{1,0:T(8,128)(2,1)}), bf16[3584,4096]{1,0:T(8,128)(2,1)}) %all-gather.10.cloned.1.call-update) | async-done | bytes 29360144 | tf_op jit(solution)/shard_map/all_gather | solution.py:23
  645.0 30.0 %fusion.3 = (bf16[128,3584]{0,1:T(8,128)(2,1)}, bf16[128,3584]{0,1:T(8,128)(2,1)}) fusion(bf16[128,3584]{0,1:T(8,128)(2,1)S(1)} %copy.22, f32[128,3584]{0,1:T(8,128)S(1)} %convolution_bitcast_fusion.1, bf16[128,4096]{1,0:T(8,128)(2,1)} %all-gather.8.cloned.1.call-done, f32[3584,4096]{1,0:T(8,128)} %bitcast.24, ...), kind=kOutput, calls=%fused_computation.14 | convolution fusion | flops 3808559104 | bytes 93716480 | tf_op jit(solution)/shard_map/td,fd->tf/dot_general | solution.py:31
  675.1 15.1 convolution_convert_fusion.1
  690.1 7.9 all-to-all-start
  698.1 14.0 convolution_convert_fusion
  712.1 658.8 %all-to-all-done = bf16[16,224,4096]{2,1,0:T(8,128)(2,1)} async-done(((bf16[16,224,4096]{2,1,0:T(8,128)(2,1)}), bf16[16,224,4096]{2,1,0:T(8,128)(2,1)}, u32[]{:S(2)}, u32[]{:S(2)}) %all-to-all-start) | async-done | bytes 29360160 | tf_op jit(solution)/shard_map/all_to_all | solution.py:49
  1370.9 6.0 all-to-all-start.1
  1376.9 0.0 reduce-scatter.2.cloned.1.call-start
  1377.0 29.8 %fusion.8 = f32[128,4096]{1,0:T(8,128)} fusion(bf16[128,3584]{0,1:T(8,128)(2,1)} %get-tuple-element.16, f32[3584,4096]{1,0:T(8,128)} %bitcast.23, bf16[3584,4096]{1,0:T(8,128)(2,1)} %all-gather.6.cloned.1.call-done), kind=kOutput, calls=%fused_computation.23 | convolution fusion | flops 3802136576 | bytes 91095040 | tf_op jit(solution)/shard_map/dot_general | solution.py:44
  1406.8 30.0 %fusion = bf16[128,4096]{1,0:T(8,128)(2,1)} fusion(f32[128,4096]{1,0:T(8,128)} %fusion.8, bf16[128,3584]{0,1:T(8,128)(2,1)S(1)} %copy.22, f32[128,3584]{0,1:T(8,128)S(1)} %convolution_bitcast_fusion.1, f32[3584,4096]{1,0:T(8,128)} %bitcast.25, bf16[3584,4096]{1,0:T(8,128)(2,1)} %all-gather.10.cloned.1.call-done), kind=kOutput, calls=%fused_computation.9 | convolution fusion | flops 3806396416 | bytes 93978624 | tf_op jit(solution)/shard_map/dot_general | solution.py:45
  1436.8 0.0 reduce-scatter.2.cloned.1.call-update
  1436.8 2.2 copy.23
  1439.0 12.6 convert_reduce_fusion.1
  1451.6 595.1 %all-to-all-done.1 = bf16[16,224,4096]{2,1,0:T(8,128)(2,1)} async-done(((bf16[16,224,4096]{2,1,0:T(8,128)(2,1)}), bf16[16,224,4096]{2,1,0:T(8,128)(2,1)}, u32[]{:S(2)}, u32[]{:S(2)}) %all-to-all-start.1) | async-done | bytes 29360160 | tf_op jit(solution)/shard_map/all_to_all | solution.py:56
  2046.7 12.0 convert_reduce_fusion
  2058.8 0.0 copy-start
  2058.8 4.4 broadcast_multiply_fusion.1
  2063.2 0.0 copy-done
  2063.2 2.2 broadcast_multiply_fusion
  2065.4 0.0 reduce-scatter.2.cloned.1.call-done
  (2 shorter events, 0.0 us)
Async XLA Ops:
  7.2 2.2 copy-start.2
  7.2 250.5 %all-gather.8.cloned.1.call-start = ((), (), s32[]{:S(2)}) async-start(), calls=%async_computation.4 | async-start | bytes 1572864 | tf_op jit(solution)/shard_map/all_gather | solution.py:15
  7.9 325.9 %all-gather.6.cloned.1.call-start = ((), (), s32[]{:S(2)}) async-start(), calls=%async_computation.3 | async-start | bytes 31195136 | tf_op jit(solution)/shard_map/all_gather | solution.py:17
  8.7 636.4 %all-gather.10.cloned.1.call-start = ((), (), s32[]{:S(2)}) async-start(), calls=%async_computation.5 | async-start | bytes 31195136 | tf_op jit(solution)/shard_map/all_gather | solution.py:23
  64.9 64.6 %copy-start.1 = (bf16[128,3584]{1,0:T(8,128)(2,1)S(1)}, bf16[128,3584]{1,0:T(8,128)(2,1)}, u32[]{:S(2)}) copy-start(bf16[128,3584]{1,0:T(8,128)(2,1)} %param.11) | copy-start | bytes 2752516
  64.9 65.2 %copy-start.3 = (f32[224,16]{0,1:T(8,128)S(1)}, f32[224,16]{0,1:T(8,128)}, u32[]{:S(2)}) copy-start(f32[224,16]{0,1:T(8,128)} %param.10) | copy-start | bytes 43012
  690.1 680.7 %all-to-all-start = ((bf16[16,224,4096]{2,1,0:T(8,128)(2,1)}), bf16[16,224,4096]{2,1,0:T(8,128)(2,1)}, u32[]{:S(2)}, u32[]{:S(2)}) async-start(bf16[16,224,4096]{2,1,0:T(8,128)(2,1)} %bitcast.29), calls=%async_computation.1 | async-start | bytes 58720256 | tf_op jit(solution)/shard_map/all_to_all | solution.py:49
  1370.9 675.9 %all-to-all-start.1 = ((bf16[16,224,4096]{2,1,0:T(8,128)(2,1)}), bf16[16,224,4096]{2,1,0:T(8,128)(2,1)}, u32[]{:S(2)}, u32[]{:S(2)}) async-start(bf16[16,224,4096]{2,1,0:T(8,128)(2,1)} %bitcast.28), calls=%async_computation.2 | async-start | bytes 58720256 | tf_op jit(solution)/shard_map/all_to_all | solution.py:56
  1376.9 688.5 %reduce-scatter.2.cloned.1.call-start = ((), (), s32[]{:S(2)}) async-start(), calls=%async_computation.6 | async-start | bytes 1572864 | tf_op jit(solution)/shard_map/reduce_scatter | solution.py:46
  2058.8 4.4 copy-start
Sparse Core Ops, SparseCore 0:
  9.5 10.2 all-gather.7
  22.5 311.3 all-gather.5
  336.5 308.4 all-gather.9
  1436.9 9.5 reduce-scatter.1
where the time goes:
time: 2070 us
  waiting for transfers between devices  1610 us (78%)
  local copies, waits for them, and re-layouts  174 us (8%)
  matrix products  150 us (7%)
  blocking collectives  76.1 us (4%)
  other arithmetic  31.2 us (2%)
    all_to_all x1, waiting for transfers between devices, per_device(): lax.all_to_all(blocked(jnp.einsum('tf,td->fd', d_gate, whole, preferred_e...  659 us
    all_to_all x1, waiting for transfers between devices, per_device(): lax.all_to_all(blocked(jnp.einsum('tf,td->fd', d_up, whole, preferred_ele...  595 us
    all_gather x1, waiting for transfers between devices, per_device(): lax.all_gather(up_codes, 'inter', axis=0, tiled=True)  280 us
    unnamed x12, local copies, waits for them, and re-layouts  132 us
    all_gather x1, waiting for transfers between devices, per_device(): lax.all_gather(gate_codes, 'inter', axis=0, tiled=True)  76.2 us
    mul x2, local copies, waits for them, and re-layouts, dequantize(): codes.astype(jnp.float32).reshape(rows, blocks, width // blocks)  41.8 us
  transfers between devices with their start and end apart: 6, of which 4 were waited for; matrix products, arithmetic and copies ran while one was open for 15% of the time, Pallas kernels for 0%

commit v1 on v0

v1 whole, which is shorter than its diff:
```python
import jax
import jax.numpy as jnp
from jax import lax
from jax.sharding import PartitionSpec as P


def dequantize(codes, scales):
    rows, width = codes.shape
    blocks = scales.shape[1]
    step = width // blocks
    parts = [
        codes[:, b * step:(b + 1) * step].astype(jnp.float32) * scales[:, b:b + 1]
        for b in range(blocks)
    ]
    return jnp.concatenate(parts, axis=1).astype(jnp.bfloat16)


def per_device(tokens, gate_codes, gate_scales, up_codes, up_scales, cotangent):
    groups = lax.axis_size("inter")
    mine = lax.all_gather(tokens, "inter", axis=0, tiled=True)
    whole = lax.all_gather(mine, "intra", axis=0, tiled=False)
    slabs, count, wide = whole.shape
    back = lax.all_to_all(cotangent, "inter", split_axis=1, concat_axis=0, tiled=True)
    w_gate = dequantize(gate_codes, gate_scales)
    w_up = dequantize(up_codes, up_scales)

    def forward(weights):
        total = None
        for s in range(slabs):
            term = lax.dot_general(
                whole[s],
                weights[:, s * wide:(s + 1) * wide],
                (((1,), (1,)), ((), ())),
                preferred_element_type=jnp.float32,
            )
            total = term if total is None else total + term
        return total

    gate = forward(w_gate)
    up = forward(w_up)
    sig = jax.nn.sigmoid(gate)
    act = gate * sig
    hidden = (act * up).astype(jnp.bfloat16)
    back = back.astype(jnp.float32)
    d_up = (back * act).astype(jnp.bfloat16)
    d_gate = (back * up * sig * (1.0 + gate * (1.0 - sig))).astype(jnp.bfloat16)
    hidden = lax.all_to_all(hidden, "inter", split_axis=0, concat_axis=1, tiled=True)

    partial_sum = jnp.dot(d_gate, w_gate, preferred_element_type=jnp.float32)
    partial_sum = partial_sum + jnp.dot(d_up, w_up, preferred_element_type=jnp.float32)
    partial_sum = lax.psum_scatter(
        partial_sum.astype(jnp.bfloat16), "intra", scatter_dimension=1, tiled=True
    )
    token_grad = lax.psum_scatter(partial_sum, "inter", scatter_dimension=0, tiled=True)

    def rows_grad(d_rows):
        terms = [
            lax.dot_general(
                d_rows, whole[s], (((0,), (0,)), ((), ())), preferred_element_type=jnp.float32
            )
            for s in range(slabs)
        ]
        return jnp.concatenate(terms, axis=1) / groups

    return (hidden, token_grad, rows_grad(d_gate), rows_grad(d_up))


def solution(mesh):
    return jax.shard_map(
        per_device,
        mesh=mesh,
        in_specs=(
            P("inter", "intra"),
            P(("intra", "inter"), None),
            P(("intra", "inter"), None),
            P(("intra", "inter"), None),
            P(("intra", "inter"), None),
            P("inter", "intra"),
        ),
        out_specs=(
            P("inter", "intra"),
            P("inter", "intra"),
            P(("intra", "inter"), None),
            P(("intra", "inter"), None),
        ),
        check_vma=False,
    )
```

time: 2070 us -> 467 us (0.23)
  waiting for transfers between devices: 1610 us -> 305 us
  local copies, waits for them, and re-layouts: 174 us -> 8.98 us
  blocking collectives: 76.1 us -> 0 us
  matrix products: 150 us -> 75.2 us
    all_to_all x2, waiting for transfers between devices: 1250 us -> 10.4 us  [the longest x1 10.4 us: per_device(): lax.all_to_all(hidden, 'inter', split_axis=0, concat_axis=1, tiled=True)]
    all_gather x3 -> x2, waiting for transfers between devices: 357 us -> 114 us  [the longest x1 114 us: per_device(): mine = lax.all_gather(tokens, 'inter', axis=0, tiled=True)]
    reduce_scatter x0 -> x1, waiting for transfers between devices: none -> 154 us  [per_device(): lax.psum_scatter(partial_sum, 'inter', scatter_dimension=0, tiled=True)]
    unnamed x12 -> x34, local copies, waits for them, and re-layouts: 132 us -> 7.87 us
    all_gather x2 -> x0, blocking collectives: 76.1 us -> none  [the longest x1 40 us: per_device(): lax.all_gather(up_scales.astype(jnp.bfloat16), 'inter', axis=0, tiled=True)]
    dot_general x4 -> x8, matrix products: 89.8 us -> 43.2 us  [the longest x4 27.5 us: forward(): lax.dot_general(whole[s], weights[:, s * wide:(s + 1) * wide], (((1,), (1...]
    mul x2 -> x0, local copies, waits for them, and re-layouts: 41.8 us -> none  [dequantize(): codes.astype(jnp.float32).reshape(rows, blocks, width // blocks)]
    unnamed x2 -> x31, other arithmetic: 0.01 us -> 40.6 us
  transfers between devices with their start and end apart: 6 -> 6, of which waited for: 4 -> 4; matrix products, arithmetic and copies ran while one was open for 15% -> 18% of each run, Pallas kernels for 0% -> 0%
where the time goes in v1:
time: 467 us; the launch traced here: 463 us
  waiting for transfers between devices  305 us (65%)
  matrix products  75.2 us (16%)
  other arithmetic  46.8 us (10%)
  between operations  14.1 us (3%)
  starting transfers between devices  13.1 us (3%)
  local copies, waits for them, and re-layouts  8.98 us (2%)
    reduce_scatter x1, waiting for transfers between devices, per_device(): lax.psum_scatter(partial_sum, 'inter', scatter_dimension=0, tiled=True)  154 us
    all_gather x1, waiting for transfers between devices, per_device(): mine = lax.all_gather(tokens, 'inter', axis=0, tiled=True)  114 us
    unnamed x31, other arithmetic  40.6 us
    dot_general x4, matrix products, forward(): lax.dot_general(whole[s], weights[:, s * wide:(s + 1) * wide], (((1,), (1...  27.5 us
    reduce_scatter x1, waiting for transfers between devices, per_device(): lax.psum_scatter(partial_sum.astype(jnp.bfloat16), 'intra', scatter_dimen...  26.3 us
    dot_general x1, matrix products, per_device(): jnp.dot(d_up, w_up, preferred_element_type=jnp.float32)  16.9 us
    dot_general x4, matrix products, rows_grad(): lax.dot_general(d_rows, whole[s], (((0,), (0,)), ((), ())), preferred_ele...  15.7 us
    dot_general x1, matrix products, per_device(): partial_sum = jnp.dot(d_gate, w_gate, preferred_element_type=jnp.float32)  15 us
  transfers between devices with their start and end apart: 6, of which 4 were waited for; matrix products, arithmetic and copies ran while one was open for 18% of the time, Pallas kernels for 0%

profile of v1, /device:TPU:28, one launch (start us, length us, event | category | flops | bytes accessed | tf_op | source)
XLA Modules:
  0.0 463.3 jit_solution(1570176110932852104)
XLA Ops:
  7.2 0.0 all-gather.4.cloned.1.call-start
  7.2 0.7 all-gather.4.cloned.1.call-update
  7.9 0.0 all-gather.6.cloned.1.call-start
  7.9 114.2 %all-gather.4.cloned.1.call-done = bf16[2048,2048]{1,0:T(8,128)(2,1)} async-done(((bf16[128,2048]{1,0:T(8,128)(2,1)}), bf16[2048,2048]{1,0:T(8,128)(2,1)}) %all-gather.4.cloned.1.call-update) | async-done | bytes 8388624 | tf_op jit(solution)/shard_map/all_gather | solution.py:20
  122.1 0.0 all-gather.6.cloned.1.call-update
  122.2 1.2 copy-done
  123.3 1.3 copy.13
  124.6 6.1 %all-to-all-start.1 = ((bf16[128,16,224]{0,2,1:T(8,128)(2,1)}), bf16[128,16,224]{0,2,1:T(8,128)(2,1)S(1)}, u32[]{:S(2)}, u32[]{:S(2)}) async-start(bf16[128,16,224]{0,2,1:T(8,128)(2,1)} %bitcast.36), calls=%async_computation.1 | async-start | bytes 1835008 | tf_op jit(solution)/shard_map/all_to_all | solution.py:23
  130.6 0.0 reduce-scatter.3.cloned.1.call-start
  130.8 1.0 constant_dynamic-update-slice_fusion.63
  131.8 1.0 constant_dynamic-update-slice_fusion.62
  132.8 1.1 constant_dynamic-update-slice_fusion.61
  133.9 1.1 constant_dynamic-update-slice_fusion.60
  135.0 1.0 constant_dynamic-update-slice_fusion.59
  136.0 1.0 constant_dynamic-update-slice_fusion.58
  137.1 1.1 constant_dynamic-update-slice_fusion.57
  138.2 1.0 constant_dynamic-update-slice_fusion.56
  139.2 0.9 copy-done.8
  140.2 1.0 constant_dynamic-update-slice_fusion.55
  141.2 1.7 constant_dynamic-update-slice_fusion.47
  142.9 1.7 constant_dynamic-update-slice_fusion.46
  144.6 1.7 constant_dynamic-update-slice_fusion.45
  146.3 1.6 constant_dynamic-update-slice_fusion.44
  148.0 1.6 constant_dynamic-update-slice_fusion.43
  149.6 1.6 constant_dynamic-update-slice_fusion.42
  151.2 1.6 constant_dynamic-update-slice_fusion.41
  152.9 1.6 constant_dynamic-update-slice_fusion.40
  154.5 1.8 constant_dynamic-update-slice_fusion.39
  156.3 1.0 constant_dynamic-update-slice_fusion.54
  157.3 1.0 constant_dynamic-update-slice_fusion.53
  158.3 1.0 constant_dynamic-update-slice_fusion.52
  159.3 1.0 constant_dynamic-update-slice_fusion.51
  160.3 1.0 constant_dynamic-update-slice_fusion.50
  161.3 1.0 constant_dynamic-update-slice_fusion.49
  162.3 1.0 constant_dynamic-update-slice_fusion.48
  163.4 0.9 copy-done.7
  164.3 1.7 constant_dynamic-update-slice_fusion.38
  165.9 1.7 constant_dynamic-update-slice_fusion.37
  167.6 1.7 constant_dynamic-update-slice_fusion.36
  169.3 1.7 constant_dynamic-update-slice_fusion.35
  171.0 1.7 constant_dynamic-update-slice_fusion.34
  172.7 1.7 constant_dynamic-update-slice_fusion.33
  174.4 1.7 constant_dynamic-update-slice_fusion.32
  176.0 7.7 %fusion.2 = f32[224,2048]{1,0:T(8,128)} fusion(bf16[224,2048]{1,0:T(8,128)(2,1)} %copy-done.7, bf16[4096,2048]{1,0:T(8,128)(2,1)} %all-gather.6.cloned.1.call-done), kind=kOutput, calls=%fused_computation.3 | convolution fusion | flops 1879048192 | bytes 11141120 | tf_op jit(solution)/shard_map/dot_general | solution.py:30
  183.8 6.7 %fusion.4 = f32[224,2048]{1,0:T(8,128)S(1)} fusion(bf16[224,2048]{1,0:T(8,128)(2,1)} %get-tuple-element.44, bf16[4096,2048]{1,0:T(8,128)(2,1)} %all-gather.6.cloned.1.call-done), kind=kOutput, calls=%fused_computation.5 | convolution fusion | flops 1879048192 | bytes 11141120 | tf_op jit(solution)/shard_map/dot_general | solution.py:30
  190.5 3.9 fusion.19
  194.3 0.9 copy-done.1
  195.3 9.3 %fusion.31 = (bf16[2048,224]{0,1:T(8,128)(2,1)S(1)}, bf16[2048,224]{0,1:T(8,128)(2,1)S(1)}, bf16[28,16,8,128]{3,2,1,0:T(8,128)(2,1)}) fusion(f32[2048,224]{0,1:T(8,128)} %fusion.19, f32[224,2048]{1,0:T(8,128)} %fusion.2, bf16[224,2048]{1,0:T(8,128)(2,1)} %copy-done.8, bf16[4096,2048]{1,0:T(8,128)(2,1)} %all-gather.6.cloned.1.call-done, ...), kind=kOutput, calls=%fused_computation.28 | convolution fusion | flops 1886846976 | bytes 16646144 | tf_op jit(solution)/shard_map/dot_general | solution.py:30
  204.5 15.0 %fusion.38 = f32[2048,4096]{1,0:T(8,128)} fusion(bf16[2048,224]{0,1:T(8,128)(2,1)S(1)} %get-tuple-element.9, bf16[224,4096]{1,0:T(8,128)(2,1)} %get-tuple-element.43), kind=kOutput, calls=%fused_computation.133 | convolution fusion | flops 3758096384 | bytes 36306944 | tf_op jit(solution)/shard_map/dot_general | solution.py:49
  219.5 16.9 %add_convert_fusion = bf16[2048,4096]{1,0:T(8,128)(2,1)} fusion(f32[2048,4096]{1,0:T(8,128)} %fusion.38, bf16[2048,224]{0,1:T(8,128)(2,1)S(1)} %get-tuple-element.8, bf16[224,4096]{1,0:T(8,128)(2,1)S(1)} %get-tuple-element.11), kind=kOutput, calls=%fused_computation | convolution fusion | flops 3774873600 | bytes 53084160 | tf_op jit(solution)/shard_map/dot_general | solution.py:50
  236.5 0.0 reduce-scatter.5.cloned.1.call-start
  236.5 26.3 %reduce-scatter.3.cloned.1.call-done = bf16[2048,2048]{1,0:T(8,128)(2,1)} async-done(((bf16[2048,4096]{1,0:T(8,128)(2,1)}), bf16[2048,2048]{1,0:T(8,128)(2,1)}) %reduce-scatter.3.cloned.1.call-update) | async-done | bytes 8388624 | tf_op jit(solution)/shard_map/reduce_scatter | solution.py:51
  262.9 1.2 copy-done.2
  264.0 1.1 copy.21
  265.1 6.9 %all-to-all-start = ((bf16[16,128,224]{1,2,0:T(8,128)(2,1)}), bf16[16,128,224]{1,2,0:T(8,128)(2,1)S(1)}, u32[]{:S(2)}, u32[]{:S(2)}) async-start(bf16[16,128,224]{1,2,0:T(8,128)(2,1)} %bitcast.73), calls=%async_computation | async-start | bytes 1835008 | tf_op jit(solution)/shard_map/all_to_all | solution.py:47
  272.1 5.9 %fusion.6 = f32[224,2048]{1,0:T(8,128)S(1)} fusion(bf16[2048,224]{0,1:T(8,128)(2,1)S(1)} %copy-done.4, bf16[4096,2048]{1,0:T(8,128)(2,1)} %all-gather.6.cloned.1.call-done), kind=kOutput, calls=%fused_computation.7 | convolution fusion | flops 1879048192 | bytes 11141120 | tf_op jit(solution)/shard_map/dot_general | solution.py:58
  277.9 5.6 %fusion.14 = f32[224,2048]{1,0:T(8,128)S(1)} fusion(bf16[2048,224]{0,1:T(8,128)(2,1)S(1)} %copy-done.4, bf16[4096,2048]{1,0:T(8,128)(2,1)} %all-gather.6.cloned.1.call-done), kind=kOutput, calls=%fused_computation.15 | convolution fusion | flops 1879048192 | bytes 11141120 | tf_op jit(solution)/shard_map/dot_general | solution.py:58
  283.6 0.2 slice-done.3
  283.8 2.1 fusion
  285.9 2.1 fusion.8
  288.0 3.5 maximum_multiply_fusion
  291.6 10.4 %all-to-all-done = bf16[16,128,224]{1,2,0:T(8,128)(2,1)S(1)} async-done(((bf16[16,128,224]{1,2,0:T(8,128)(2,1)}), bf16[16,128,224]{1,2,0:T(8,128)(2,1)S(1)}, u32[]{:S(2)}, u32[]{:S(2)}) %all-to-all-start) | async-done | bytes 917536 | tf_op jit(solution)/shard_map/all_to_all | solution.py:47
  302.0 1.3 copy.15
  303.3 153.5 %reduce-scatter.5.cloned.1.call-done = bf16[128,2048]{1,0:T(8,128)(2,1)} async-done(((bf16[2048,2048]{1,0:T(8,128)(2,1)}), bf16[128,2048]{1,0:T(8,128)(2,1)}) %reduce-scatter.5.cloned.1.call-update) | async-done | bytes 524304 | tf_op jit(solution)/shard_map/reduce_scatter | solution.py:54
  (33 shorter events, 0.1 us)
Async XLA Ops:
  7.2 115.0 %all-gather.4.cloned.1.call-start = ((), (), s32[]{:S(2)}) async-start(), calls=%async_computation.4 | async-start | bytes 8912896 | tf_op jit(solution)/shard_map/all_gather | solution.py:20
  7.9 168.1 %all-gather.6.cloned.1.call-start = ((), (), s32[]{:S(2)}) async-start(), calls=%async_computation.7 | async-start | bytes 25165824 | tf_op jit(solution)/shard_map/all_gather | solution.py:21
  122.1 1.2 copy-start
  123.3 7.4 %copy-start.5 = (f32[224,16]{0,1:T(8,128)S(1)}, f32[224,16]{0,1:T(8,128)}, u32[]{:S(2)}) copy-start(f32[224,16]{0,1:T(8,128)} %param.8) | copy-start | bytes 43012
  123.3 7.4 %copy-start.6 = (f32[224,16]{0,1:T(8,128)S(1)}, f32[224,16]{0,1:T(8,128)}, u32[]{:S(2)}) copy-start(f32[224,16]{0,1:T(8,128)} %param.10) | copy-start | bytes 43012
  124.6 69.8 %all-to-all-start.1 = ((bf16[128,16,224]{0,2,1:T(8,128)(2,1)}), bf16[128,16,224]{0,2,1:T(8,128)(2,1)S(1)}, u32[]{:S(2)}, u32[]{:S(2)}) async-start(bf16[128,16,224]{0,2,1:T(8,128)(2,1)} %bitcast.36), calls=%async_computation.1 | async-start | bytes 1835008 | tf_op jit(solution)/shard_map/all_to_all | solution.py:23
  130.6 132.2 %reduce-scatter.3.cloned.1.call-start = ((), (), s32[]{:S(2)}) async-start(), calls=%async_computation.5 | async-start | bytes 25165824 | tf_op jit(solution)/shard_map/reduce_scatter | solution.py:51
  139.2 1.0 copy-start.8
  154.5 14.8 %copy-start.9 = (bf16[224,2048]{1,0:T(8,128)(2,1)}, bf16[224,2048]{1,0:T(8,128)(2,1)S(1)}, u32[]{:S(2)}) copy-start(bf16[224,2048]{1,0:T(8,128)(2,1)S(1)} %get-tuple-element.60) | copy-start | bytes 2752516
  163.3 0.9 copy-start.7
  176.0 14.4 %copy-start.11 = (bf16[4096,2048]{1,0:T(8,128)(2,1)S(1)}, bf16[4096,2048]{1,0:T(8,128)(2,1)}, u32[]{:S(2)}) copy-start(bf16[4096,2048]{1,0:T(8,128)(2,1)} %all-gather.6.cloned.1.call-done) | copy-start | bytes 50331652
  183.8 6.7 %copy-start.10 = (bf16[224,2048]{1,0:T(8,128)(2,1)S(1)}, bf16[224,2048]{1,0:T(8,128)(2,1)}, u32[]{:S(2)}) copy-start(bf16[224,2048]{1,0:T(8,128)(2,1)} %copy-done.9) | copy-start | bytes 2752516
  194.3 0.9 copy-start.1
  204.5 15.0 %copy-start.3 = (bf16[2048,224]{0,1:T(8,128)(2,1)}, bf16[2048,224]{0,1:T(8,128)(2,1)S(1)}, u32[]{:S(2)}) copy-start(bf16[2048,224]{0,1:T(8,128)(2,1)S(1)} %get-tuple-element.8) | copy-start | bytes 2752516
  236.5 220.3 %reduce-scatter.5.cloned.1.call-start = ((), (), s32[]{:S(2)}) async-start(), calls=%async_computation.6 | async-start | bytes 8912896 | tf_op jit(solution)/shard_map/reduce_scatter | solution.py:54
  262.9 1.2 copy-start.2
  264.0 8.0 %copy-start.4 = (bf16[2048,224]{0,1:T(8,128)(2,1)S(1)}, bf16[2048,224]{0,1:T(8,128)(2,1)}, u32[]{:S(2)}) copy-start(bf16[2048,224]{0,1:T(8,128)(2,1)} %copy-done.3) | copy-start | bytes 2752516
  265.1 36.9 %all-to-all-start = ((bf16[16,128,224]{1,2,0:T(8,128)(2,1)}), bf16[16,128,224]{1,2,0:T(8,128)(2,1)S(1)}, u32[]{:S(2)}, u32[]{:S(2)}) async-start(bf16[16,128,224]{1,2,0:T(8,128)(2,1)} %bitcast.73), calls=%async_computation | async-start | bytes 1835008 | tf_op jit(solution)/shard_map/all_to_all | solution.py:47
  272.0 11.5 %slice-start = ((s8[16777216]{0:T(1024)(128)(4,1)}), s8[4194304]{0:T(1024)(128)(4,1)S(1)}, s32[]{:S(2)}) async-start(s8[16777216]{0:T(1024)(128)(4,1)} %bitcast.107), calls=%async_computation.8 | async-start | bytes 8388608
  272.0 11.5 %slice-start.1 = ((s8[16777216]{0:T(1024)(128)(4,1)}), s8[4194304]{0:T(1024)(128)(4,1)S(1)}, s32[]{:S(2)}) async-start(s8[16777216]{0:T(1024)(128)(4,1)} %bitcast.107), calls=%async_computation.9 | async-start | bytes 8388608
  277.9 5.6 %slice-start.2 = ((s8[16777216]{0:T(1024)(128)(4,1)}), s8[4194304]{0:T(1024)(128)(4,1)S(1)}, s32[]{:S(2)}) async-start(s8[16777216]{0:T(1024)(128)(4,1)} %bitcast.107), calls=%async_computation.10 | async-start | bytes 8388608
  277.9 5.8 %slice-start.3 = ((s8[16777216]{0:T(1024)(128)(4,1)}), s8[4194304]{0:T(1024)(128)(4,1)S(1)}, s32[]{:S(2)}) async-start(s8[16777216]{0:T(1024)(128)(4,1)} %bitcast.107), calls=%async_computation.11 | async-start | bytes 8388608
Sparse Core Ops, SparseCore 0:
  10.7 111.3 all-gather.3
  123.7 30.3 all-gather.5
  236.6 26.2 reduce-scatter.2
  265.6 191.1 reduce-scatter.4

commit v2 on v1

--- a/solution.py
+++ b/solution.py
@@ -1,7 +1,264 @@
+import functools
+
 import jax
 import jax.numpy as jnp
 from jax import lax
+from jax.experimental import pallas as pl
+from jax.experimental.pallas import tpu as pltpu
 from jax.sharding import PartitionSpec as P
+
+MESH = pl.DeviceIdType.MESH
+
+
+def place(groups):
+    me = lax.axis_index("inter")
+    core = lax.axis_index("intra")
+    line = groups // 4
+    return me, core, me // 4, line
+
+
+def bits(me, parity):
+    low, high = me % 2, (me // 2) % 2
+    a = low * (1 - parity) + high * parity
+    b = high * (1 - parity) + low * parity
+    return a, b, 1 + parity, 2 - parity
+
+
+def block_of(z, a, b, stride_a, stride_b):
+    return z * 4 + a * stride_a + b * stride_b
+
+
+def greet(peers):
+    barrier = pltpu.get_barrier_semaphore()
+    for peer in peers:
+        pl.semaphore_signal(barrier, inc=1, device_id=peer, device_id_type=MESH)
+    pl.semaphore_wait(barrier, len(peers))
+
+
+def peers_of(me, core, z, line, cores, a, b, sa, sb):
+    to_a = {"inter": block_of(z, 1 - a, b, sa, sb)}
+    to_b = {"inter": block_of(z, a, 1 - b, sa, sb)}
+    to_z = [{"inter": block_of(lax.rem(z + j, line), a, b, sa, sb)} for j in range(1, line)]
+    to_core = [{"intra": lax.rem(core + i, cores)} for i in range(1, cores)]
+    return to_a, to_b, to_z, to_core
+
+
+def gather_kernel(groups, cores, x_ref, out_ref, own_sem, *sems):
+    me, core, z, line = place(groups)
+    a, b, sa, sb = bits(me, core % 2)
+    rows = x_ref.shape[0]
+    to_a, to_b, to_z, to_core = peers_of(me, core, z, line, cores, a, b, sa, sb)
+    greet([to_a, to_b] + to_z + to_core)
+    z_send, z_recv, b_send, b_recv, a_send, a_recv, c_send, c_recv = sems
+
+    def at(slab, block):
+        return out_ref.at[slab, pl.ds(pl.multiple_of(block * rows, rows), rows), :]
+
+    started = []
+
+    def send(src, block, send_sem, recv_sem, peer):
+        copy = pltpu.make_async_remote_copy(
+            src_ref=src, dst_ref=at(core, block), send_sem=send_sem, recv_sem=recv_sem,
+            device_id=peer, device_id_type=MESH,
+        )
+        copy.start()
+        started.append(copy)
+
+    def arrived(slab, block, send_sem, recv_sem, peer):
+        pltpu.make_async_remote_copy(
+            src_ref=x_ref, dst_ref=at(slab, block), send_sem=send_sem, recv_sem=recv_sem,
+            device_id=peer, device_id_type=MESH,
+        ).wait_recv()
+
+    def to_cores(src, block, slot):
+        for i, peer in enumerate(to_core):
+            send(src, block, c_send.at[i, slot], c_recv.at[i, slot], peer)
+
+    own = pltpu.make_async_copy(x_ref, at(core, me), own_sem)
+    for j in range(1, line):
+        send(x_ref, me, z_send.at[j - 1], z_recv.at[j - 1], to_z[j - 1])
+    send(x_ref, me, b_send.at[0], b_recv.at[0], to_b)
+    send(x_ref, me, a_send.at[0], a_recv.at[0], to_a)
+    to_cores(x_ref, me, 0)
+    own.start()
+
+    def take_a(j):
+        zz = lax.rem(z - j + line, line)
+        for k, bb in ((2, b), (3, 1 - b)):
+            block = block_of(zz, 1 - a, bb, sa, sb)
+            slot = (k - 2) * line + j
+            arrived(core, block, a_send.at[slot], a_recv.at[slot], to_a)
+            to_cores(at(core, block), block, k * line + j)
+
+    for j in range(line):
+        zz = lax.rem(z - j + line, line)
+        if j > 0:
+            block = block_of(zz, a, b, sa, sb)
+            arrived(core, block, z_send.at[j - 1], z_recv.at[j - 1], to_z[j - 1])
+            send(at(core, block), block, b_send.at[j], b_recv.at[j], to_b)
+            send(at(core, block), block, a_send.at[j], a_recv.at[j], to_a)
+            to_cores(at(core, block), block, j)
+        block = block_of(zz, a, 1 - b, sa, sb)
+        arrived(core, block, b_send.at[j], b_recv.at[j], to_b)
+        send(at(core, block), block, a_send.at[line + j], a_recv.at[line + j], to_a)
+        to_cores(at(core, block), block, line + j)
+        if j > 0:
+            take_a(j - 1)
+    take_a(line - 1)
+    for i in range(1, cores):
+        other = lax.rem(core - i + cores, cores)
+        oa, ob, osa, osb = bits(me, other % 2)
+        for k, (da, db) in enumerate(((0, 0), (0, 1), (1, 0), (1, 1))):
+            aa = oa + da - 2 * da * oa
+            bb = ob + db - 2 * db * ob
+            for j in range(line):
+                zz = lax.rem(z - j + line, line)
+                block = block_of(zz, aa, bb, osa, osb)
+                slot = k * line + j
+                arrived(other, block, c_send.at[i - 1, slot], c_recv.at[i - 1, slot], to_core[i - 1])
+    own.wait()
+    for copy in started:
+        copy.wait_send()
+
+
+def gather_tokens(tokens, groups, cores):
+    rows, wide = tokens.shape
+    line = groups // 4
+    dma = pltpu.SemaphoreType.DMA
+    return pl.pallas_call(
+        functools.partial(gather_kernel, groups, cores),
+        out_shape=jax.ShapeDtypeStruct((cores, groups * rows, wide), tokens.dtype),
+        in_specs=[pl.BlockSpec(memory_space=pl.ANY)],
+        out_specs=pl.BlockSpec(memory_space=pl.ANY),
+        scratch_shapes=[
+            dma,
+            dma((line - 1,)), dma((line - 1,)),
+            dma((line,)), dma((line,)),
+            dma((2 * line,)), dma((2 * line,)),
+            dma((cores - 1, 4 * line)), dma((cores - 1, 4 * line)),
+        ],
+        compiler_params=pltpu.CompilerParams(collective_id=0, has_side_effects=True),
+        name="gather_tokens",
+    )(tokens)
+
+
+def scatter_kernel(groups, cores, x_ref, out_ref, acc, from_core, from_a, from_b, from_z, *sems):
+    me, core, z, line = place(groups)
+    a, b, sa, sb = bits(me, core % 2)
+    rows, wide = out_ref.shape
+    to_a, to_b, to_z, to_core = peers_of(me, core, z, line, cores, a, b, sa, sb)
+    greet([to_a, to_b] + to_z + to_core)
+    own_sem, c_send, c_recv, a_send, a_recv, b_send, b_recv, z_send, z_recv = sems
+
+    def block_at(parity, k, j):
+        pa, pb, psa, psb = bits(me, parity)
+        aa = 1 - pa if k < 2 else pa
+        bb = 1 - pb if k % 2 == 0 else pb
+        return block_of(lax.rem(z + 1 + j, line), aa, bb, psa, psb)
+
+    def part(block, slab):
+        return x_ref.at[
+            pl.ds(pl.multiple_of(block * rows, rows), rows),
+            pl.ds(pl.multiple_of(slab * wide, wide), wide),
+        ]
+
+    started, loads = [], {}
+
+    def remote(src, dst, send_sem, recv_sem, peer):
+        return pltpu.make_async_remote_copy(
+            src_ref=src, dst_ref=dst, send_sem=send_sem, recv_sem=recv_sem,
+            device_id=peer, device_id_type=MESH,
+        )
+
+    def send(*args):
+        copy = remote(*args)
+        copy.start()
+        started.append(copy)
+
+    for k in range(4):
+        for j in range(line):
+            slot = k * line + j
+            for i in range(1, cores):
+                other = lax.rem(core + i, cores)
+                block = block_at(other % 2, k, j)
+                send(part(block, other), from_core.at[i - 1, slot], c_send.at[i - 1, slot],
+                     c_recv.at[i - 1, slot], to_core[i - 1])
+            loads[slot] = pltpu.make_async_copy(
+                part(block_at(core % 2, k, j), core), acc.at[slot], own_sem.at[slot])
+            loads[slot].start()
+
+    def group_sum(slot, extras):
+        loads[slot].wait()
+        for i in range(cores - 1):
+            remote(acc.at[slot], from_core.at[i, slot], c_send.at[i, slot], c_recv.at[i, slot],
+                   to_core[i]).wait_recv()
+        refs = [acc.at[slot]] + [from_core.at[i, slot] for i in range(cores - 1)] + extras
+        return refs
+
+    def add(refs, dst):
+        step = 16
+
+        def body(r, _):
+            here = pl.ds(pl.multiple_of(r * step, step), step)
+            total = refs[0][here, :].astype(jnp.float32)
+            for ref in refs[1:]:
+                total = total + ref[here, :].astype(jnp.float32)
+            dst[here, :] = total.astype(dst.dtype)
+            return 0
+
+        lax.fori_loop(0, rows // step, body, 0)
+
+    for slot in range(2 * line):
+        add(group_sum(slot, []), acc.at[slot])
+        send(acc.at[slot], from_a.at[slot], a_send.at[slot], a_recv.at[slot], to_a)
+    for j in range(line):
+        slot = 2 * line + j
+        refs = group_sum(slot, [from_a.at[j]])
+        remote(acc.at[slot], from_a.at[j], a_send.at[j], a_recv.at[j], to_a).wait_recv()
+        add(refs, acc.at[slot])
+        send(acc.at[slot], from_b.at[j], b_send.at[j], b_recv.at[j], to_b)
+    for j in range(line):
+        slot = 3 * line + j
+        refs = group_sum(slot, [from_a.at[line + j], from_b.at[j]])
+        remote(acc.at[slot], from_a.at[line + j], a_send.at[line + j], a_recv.at[line + j],
+               to_a).wait_recv()
+        remote(acc.at[slot], from_b.at[j], b_send.at[j], b_recv.at[j], to_b).wait_recv()
+        if j < line - 1:
+            add(refs, acc.at[slot])
+            send(acc.at[slot], from_z.at[j], z_send.at[j], z_recv.at[j], to_z[j])
+        else:
+            for i in range(line - 1):
+                remote(acc.at[slot], from_z.at[i], z_send.at[i], z_recv.at[i], to_z[i]).wait_recv()
+            add(refs + [from_z.at[i] for i in range(line - 1)], out_ref)
+    for copy in started:
+        copy.wait_send()
+
+
+def scatter_sum(partial_sum, groups, cores):
+    tokens, width = partial_sum.shape
+    rows, wide, line = tokens // groups, width // cores, groups // 4
+    dma = pltpu.SemaphoreType.DMA
+
+    def slots(*count):
+        return pltpu.VMEM((*count, rows, wide), partial_sum.dtype)
+
+    return pl.pallas_call(
+        functools.partial(scatter_kernel, groups, cores),
+        out_shape=jax.ShapeDtypeStruct((rows, wide), partial_sum.dtype),
+        in_specs=[pl.BlockSpec(memory_space=pl.ANY)],
+        out_specs=pl.BlockSpec(memory_space=pltpu.VMEM),
+        scratch_shapes=[
+            slots(4 * line), slots(cores - 1, 4 * line), slots(2 * line), slots(line),
+            slots(line - 1),
+            dma((4 * line,)),
+            dma((cores - 1, 4 * line)), dma((cores - 1, 4 * line)),
+            dma((2 * line,)), dma((2 * line,)),
+            dma((line,)), dma((line,)),
+            dma((line - 1,)), dma((line - 1,)),
+        ],
+        compiler_params=pltpu.CompilerParams(collective_id=1, has_side_effects=True),
+        name="scatter_sum",
+    )(partial_sum)
 
 
 def dequantize(codes, scales):
@@ -17,8 +274,7 @@
 
 def per_device(tokens, gate_codes, gate_scales, up_codes, up_scales, cotangent):
     groups = lax.axis_size("inter")
-    mine = lax.all_gather(tokens, "inter", axis=0, tiled=True)
-    whole = lax.all_gather(mine, "intra", axis=0, tiled=False)
+    whole = gather_tokens(tokens, groups, lax.axis_size("intra"))
     slabs, count, wide = whole.shape
     back = lax.all_to_all(cotangent, "inter", split_axis=1, concat_axis=0, tiled=True)
     w_gate = dequantize(gate_codes, gate_scales)
@@ -48,10 +304,9 @@
 
     partial_sum = jnp.dot(d_gate, w_gate, preferred_element_type=jnp.float32)
     partial_sum = partial_sum + jnp.dot(d_up, w_up, preferred_element_type=jnp.float32)
-    partial_sum = lax.psum_scatter(
-        partial_sum.astype(jnp.bfloat16), "intra", scatter_dimension=1, tiled=True
+    token_grad = scatter_sum(
+        partial_sum.astype(jnp.bfloat16), groups, lax.axis_size("intra")
     )
-    token_grad = lax.psum_scatter(partial_sum, "inter", scatter_dimension=0, tiled=True)
 
     def rows_grad(d_rows):
         terms = [

time: 467 us -> 352 us (0.75)
  waiting for transfers between devices: 305 us -> 0.01 us
  Pallas kernels: 0 us -> 207 us
  between operations: 14.1 us -> 1.1 us
  other arithmetic: 46.8 us -> 36 us
  matrix products: 75.2 us -> 80.9 us
  starting transfers between devices: 13.1 us -> 17.9 us
    pallas_call x0 -> x2, Pallas kernels: none -> 207 us  [the longest x1 104 us: gather_tokens(): pl.pallas_call(functools.partial(gather_kernel, groups, cores), out_shape...]
    reduce_scatter x2 -> x0, waiting for transfers between devices: 180 us -> none  [the longest x1 154 us: per_device(): lax.psum_scatter(partial_sum, 'inter', scatter_dimension=0, tiled=True)]
    all_gather x2 -> x0, waiting for transfers between devices: 114 us -> none  [the longest x1 114 us: per_device(): mine = lax.all_gather(tokens, 'inter', axis=0, tiled=True)]
    all_to_all x1, waiting for transfers between devices: 10.4 us -> 0.01 us  [per_device(): lax.all_to_all(hidden, 'inter', split_axis=0, concat_axis=1, tiled=True)]
    unnamed x31, other arithmetic: 40.6 us -> 30.4 us
    dot_general x4, matrix products: 15.7 us -> 23.3 us  [rows_grad(): lax.dot_general(d_rows, whole[s], (((0,), (0,)), ((), ())), preferred_ele...]
  transfers between devices with their start and end apart: 6 -> 2, of which waited for: 4 -> 0; matrix products, arithmetic and copies ran while one was open for 18% -> 28% of each run, Pallas kernels for 0% -> 59%
where the time goes in v2:
time: 352 us; the launch traced here: 348 us
  Pallas kernels  207 us (59%)
  matrix products  80.9 us (23%)
  other arithmetic  36 us (10%)
  starting transfers between devices  17.9 us (5%)
  local copies, waits for them, and re-layouts  5.48 us (2%)
    pallas_call x1, Pallas kernels, gather_tokens(): pl.pallas_call(functools.partial(gather_kernel, groups, cores), out_shape...  104 us
    pallas_call x1, Pallas kernels, scatter_sum(): pl.pallas_call(functools.partial(scatter_kernel, groups, cores), out_shap...  102 us
    unnamed x31, other arithmetic  30.4 us
    dot_general x4, matrix products, rows_grad(): lax.dot_general(d_rows, whole[s], (((0,), (0,)), ((), ())), preferred_ele...  23.3 us
    dot_general x4, matrix products, forward(): lax.dot_general(whole[s], weights[:, s * wide:(s + 1) * wide], (((1,), (1...  23.1 us
    dot_general x1, matrix products, per_device(): partial_sum = jnp.dot(d_gate, w_gate, preferred_element_type=jnp.float32)  17.5 us
    dot_general x1, matrix products, per_device(): jnp.dot(d_up, w_up, preferred_element_type=jnp.float32)  17 us
    all_to_all x1, starting transfers between devices, per_device(): lax.all_to_all(hidden, 'inter', split_axis=0, concat_axis=1, tiled=True)  10.9 us
  transfers between devices with their start and end apart: 2, of which 0 were waited for; matrix products, arithmetic and copies ran while one was open for 28% of the time, Pallas kernels for 59%

profile of v2, /device:TPU:28, one launch (start us, length us, event | category | flops | bytes accessed | tf_op | source)
XLA Modules:
  0.0 348.0 jit_solution(17045902660715125689)
XLA Ops:
  0.6 0.0 copy-start.9
  0.6 0.0 copy-start.10
  0.7 2.2 copy.13
  2.9 6.9 %all-to-all-start.1 = ((bf16[128,16,224]{0,2,1:T(8,128)(2,1)}), bf16[128,16,224]{0,2,1:T(8,128)(2,1)S(1)}, u32[]{:S(2)}, u32[]{:S(2)}) async-start(bf16[128,16,224]{0,2,1:T(8,128)(2,1)} %bitcast.38), calls=%async_computation.1 | async-start | bytes 1835008 | tf_op jit(solution)/shard_map/all_to_all | solution.py:279
  9.8 0.0 copy-done.9
  9.9 0.0 copy-done.10
  9.9 104.2 %gather_tokens.1 = bf16[2,2048,2048]{2,1,0:T(8,128)(2,1)} custom-call(bf16[128,2048]{1,0:T(8,128)(2,1)} %x_ref.1), custom_call_target="tpu_custom_call" | custom-call | tf_op jit(solution)/shard_map/gather_tokens/pallas_call | solution.py:128
  114.1 1.0 constant_dynamic-update-slice_fusion.63
  115.1 1.0 constant_dynamic-update-slice_fusion.62
  116.1 1.0 constant_dynamic-update-slice_fusion.61
  117.1 1.0 constant_dynamic-update-slice_fusion.60
  118.1 1.0 constant_dynamic-update-slice_fusion.59
  119.1 1.0 constant_dynamic-update-slice_fusion.58
  120.1 1.0 constant_dynamic-update-slice_fusion.57
  121.2 1.0 constant_dynamic-update-slice_fusion.56
  122.2 0.0 copy-start.11
  122.2 1.1 constant_dynamic-update-slice_fusion.55
  123.3 1.0 constant_dynamic-update-slice_fusion.47
  124.3 1.0 constant_dynamic-update-slice_fusion.46
  125.3 1.0 constant_dynamic-update-slice_fusion.45
  126.3 1.0 constant_dynamic-update-slice_fusion.44
  127.3 1.0 constant_dynamic-update-slice_fusion.43
  128.3 1.0 constant_dynamic-update-slice_fusion.42
  129.4 1.0 constant_dynamic-update-slice_fusion.41
  130.4 1.0 constant_dynamic-update-slice_fusion.40
  131.4 1.0 constant_dynamic-update-slice_fusion.39
  132.4 1.0 constant_dynamic-update-slice_fusion.54
  133.4 0.0 copy-done.11
  133.4 1.0 constant_dynamic-update-slice_fusion.53
  134.4 1.0 constant_dynamic-update-slice_fusion.52
  135.4 1.0 constant_dynamic-update-slice_fusion.51
  136.4 1.0 constant_dynamic-update-slice_fusion.50
  137.4 1.0 constant_dynamic-update-slice_fusion.49
  138.4 1.0 constant_dynamic-update-slice_fusion.48
  139.4 0.0 copy-start
  139.4 7.5 %fusion.4 = f32[224,2048]{1,0:T(8,128)} fusion(bf16[224,2048]{1,0:T(8,128)(2,1)S(1)} %get-tuple-element.12, bf16[2,2048,2048]{2,1,0:T(8,128)(2,1)} %gather_tokens.1), kind=kOutput, calls=%fused_computation.5 | convolution fusion | flops 1879048192 | bytes 11141120 | tf_op jit(solution)/shard_map/dot_general | solution.py:286
  146.9 1.3 constant_dynamic-update-slice_fusion.38
  148.2 1.0 constant_dynamic-update-slice_fusion.37
  149.2 1.0 constant_dynamic-update-slice_fusion.36
  150.3 1.0 constant_dynamic-update-slice_fusion.35
  151.3 1.0 constant_dynamic-update-slice_fusion.34
  152.3 1.0 constant_dynamic-update-slice_fusion.33
  153.3 1.0 constant_dynamic-update-slice_fusion.32
  154.3 0.0 copy-start.2
  154.3 0.0 copy-done
  154.3 2.6 fusion.6
  156.9 3.9 %fusion.27 = f32[2048,224]{0,1:T(8,128)} fusion(f32[224,2048]{1,0:T(8,128)S(1)} %fusion.6, bf16[224,2048]{1,0:T(8,128)(2,1)S(1)} %get-tuple-element.60, bf16[2,2048,2048]{2,1,0:T(8,128)(2,1)S(1)} %copy-done), kind=kOutput, calls=%fused_computation.28 | convolution fusion | flops 1879506944 | bytes 12976128 | tf_op jit(solution)/shard_map/dot_general | solution.py:286
  160.8 0.0 all-to-all-done.1
  160.8 9.2 %fusion.39 = (bf16[2048,224]{0,1:T(8,128)(2,1)S(1)}, bf16[2048,224]{0,1:T(8,128)(2,1)}, bf16[28,16,8,128]{3,2,1,0:T(8,128)(2,1)S(1)}) fusion(f32[2048,224]{0,1:T(8,128)} %fusion.27, f32[224,2048]{1,0:T(8,128)} %fusion.4, bf16[224,2048]{1,0:T(8,128)(2,1)} %copy-done.11, bf16[2,2048,2048]{2,1,0:T(8,128)(2,1)} %gather_tokens.1, ...), kind=kOutput, calls=%fused_computation.36 | convolution fusion | flops 1886846976 | bytes 16646144 | tf_op jit(solution)/shard_map/dot_general | solution.py:286
  170.0 7.3 %fusion = f32[224,2048]{1,0:T(8,128)} fusion(bf16[2048,224]{0,1:T(8,128)(2,1)S(1)} %get-tuple-element.8, bf16[2,2048,2048]{2,1,0:T(8,128)(2,1)} %gather_tokens.1), kind=kOutput, calls=%fused_computation.1 | convolution fusion | flops 1879048192 | bytes 11141120 | tf_op jit(solution)/shard_map/dot_general | solution.py:313
  177.3 3.4 fusion.8
  180.7 1.1 copy.21
  181.8 10.9 %all-to-all-start = ((bf16[16,128,224]{1,2,0:T(8,128)(2,1)}), bf16[16,128,224]{1,2,0:T(8,128)(2,1)S(1)}, u32[]{:S(2)}, u32[]{:S(2)}) async-start(bf16[16,128,224]{1,2,0:T(8,128)(2,1)} %bitcast.101), calls=%async_computation | async-start | bytes 1835008 | tf_op jit(solution)/shard_map/all_to_all | solution.py:303
  192.7 17.5 %fusion.46 = f32[2048,4096]{1,0:T(8,128)} fusion(bf16[2048,224]{0,1:T(8,128)(2,1)} %get-tuple-element.9, bf16[224,4096]{1,0:T(8,128)(2,1)} %copy-done.2), kind=kOutput, calls=%fused_computation.141 | convolution fusion | flops 3758096384 | bytes 36306944 | tf_op jit(solution)/shard_map/dot_general | solution.py:305
  210.2 17.0 %add_convert_fusion.x_ref = bf16[2048,4096]{1,0:T(8,128)(2,1)} fusion(f32[2048,4096]{1,0:T(8,128)} %fusion.46, bf16[2048,224]{0,1:T(8,128)(2,1)S(1)} %copy-done.8, bf16[224,4096]{1,0:T(8,128)(2,1)S(1)} %get-tuple-element.11), kind=kOutput, calls=%fused_computation | convolution fusion | flops 3774873600 | bytes 53084160 | tf_op jit(solution)/shard_map/dot_general | solution.py:306
  227.2 6.7 %fusion.2 = f32[224,2048]{1,0:T(8,128)} fusion(bf16[2048,224]{0,1:T(8,128)(2,1)S(1)} %copy-done.6, bf16[2,2048,2048]{2,1,0:T(8,128)(2,1)} %gather_tokens.1), kind=kOutput, calls=%fused_computation.3 | convolution fusion | flops 1879048192 | bytes 11141120 | tf_op jit(solution)/shard_map/dot_general | solution.py:313
  233.9 102.4 %scatter_sum.1 = bf16[128,2048]{1,0:T(8,128)(2,1)} custom-call(bf16[2048,4096]{1,0:T(8,128)(2,1)} %add_convert_fusion.x_ref), custom_call_target="tpu_custom_call" | custom-call | tf_op jit(solution)/shard_map/scatter_sum/pallas_call | solution.py:245
  336.4 0.0 copy-start.3
  336.4 0.0 copy-start.5
  336.4 5.9 %fusion.10 = f32[224,2048]{1,0:T(8,128)S(1)} fusion(bf16[2048,224]{0,1:T(8,128)(2,1)} %get-tuple-element.9, bf16[2,2048,2048]{2,1,0:T(8,128)(2,1)} %gather_tokens.1), kind=kOutput, calls=%fused_computation.11 | convolution fusion | flops 1879048192 | bytes 11141120 | tf_op jit(solution)/shard_map/dot_general | solution.py:313
  342.3 3.6 %maximum_multiply_fusion = (f32[224,4096]{1,0:T(8,128)}, f32[224,4096]{1,0:T(8,128)}) fusion(f32[224,2048]{1,0:T(8,128)S(1)} %copy-done.5, f32[224,2048]{1,0:T(8,128)S(1)} %fusion.10, f32[224,2048]{1,0:T(8,128)S(1)} %copy-done.3, f32[224,2048]{1,0:T(8,128)S(1)} %copy-done.4), kind=kLoop, calls=%fused_computation.25 | loop fusion | flops 3670016 | bytes 14680064 | tf_op jit(solution)/shard_map/div | solution.py:318
  345.9 0.0 all-to-all-done
  346.0 1.3 copy.15
  347.2 0.8 copy.81
  (24 shorter events, 0.1 us)
Async XLA Ops:
  0.6 9.2 %copy-start.9 = (f32[224,16]{0,1:T(8,128)S(1)}, f32[224,16]{0,1:T(8,128)}, u32[]{:S(2)}) copy-start(f32[224,16]{0,1:T(8,128)} %param.8) | copy-start | bytes 43012
  0.6 9.2 %copy-start.10 = (f32[224,16]{0,1:T(8,128)S(1)}, f32[224,16]{0,1:T(8,128)}, u32[]{:S(2)}) copy-start(f32[224,16]{0,1:T(8,128)} %param.10) | copy-start | bytes 43012
  2.9 157.9 %all-to-all-start.1 = ((bf16[128,16,224]{0,2,1:T(8,128)(2,1)}), bf16[128,16,224]{0,2,1:T(8,128)(2,1)S(1)}, u32[]{:S(2)}, u32[]{:S(2)}) async-start(bf16[128,16,224]{0,2,1:T(8,128)(2,1)} %bitcast.38), calls=%async_computation.1 | async-start | bytes 1835008 | tf_op jit(solution)/shard_map/all_to_all | solution.py:279
  122.2 11.2 %copy-start.11 = (bf16[224,2048]{1,0:T(8,128)(2,1)}, bf16[224,2048]{1,0:T(8,128)(2,1)S(1)}, u32[]{:S(2)}) copy-start(bf16[224,2048]{1,0:T(8,128)(2,1)S(1)} %get-tuple-element.28) | copy-start | bytes 2752516
  139.4 14.9 %copy-start = (bf16[2,2048,2048]{2,1,0:T(8,128)(2,1)S(1)}, bf16[2,2048,2048]{2,1,0:T(8,128)(2,1)}, u32[]{:S(2)}) copy-start(bf16[2,2048,2048]{2,1,0:T(8,128)(2,1)} %gather_tokens.1) | copy-start | bytes 50331652
  154.3 2.7 copy-start.2
  160.8 16.5 %slice-start = ((s8[16777216]{0:T(1024)(128)(4,1)}), s8[4194304]{0:T(1024)(128)(4,1)S(1)}, s32[]{:S(2)}) async-start(s8[16777216]{0:T(1024)(128)(4,1)} %bitcast.102), calls=%async_computation.2 | async-start | bytes 8388608
  160.8 16.5 %slice-start.1 = ((s8[16777216]{0:T(1024)(128)(4,1)}), s8[4194304]{0:T(1024)(128)(4,1)S(1)}, s32[]{:S(2)}) async-start(s8[16777216]{0:T(1024)(128)(4,1)} %bitcast.102), calls=%async_computation.3 | async-start | bytes 8388608
  160.8 16.5 %slice-start.2 = ((s8[16777216]{0:T(1024)(128)(4,1)}), s8[4194304]{0:T(1024)(128)(4,1)S(1)}, s32[]{:S(2)}) async-start(s8[16777216]{0:T(1024)(128)(4,1)} %bitcast.102), calls=%async_computation.4 | async-start | bytes 8388608
  170.0 7.3 %copy-start.7 = (bf16[2048,224]{0,1:T(8,128)(2,1)}, bf16[2048,224]{0,1:T(8,128)(2,1)S(1)}, u32[]{:S(2)}) copy-start(bf16[2048,224]{0,1:T(8,128)(2,1)S(1)} %get-tuple-element.8) | copy-start | bytes 2752516
  170.0 7.3 %slice-start.3 = ((s8[16777216]{0:T(1024)(128)(4,1)}), s8[4194304]{0:T(1024)(128)(4,1)S(1)}, s32[]{:S(2)}) async-start(s8[16777216]{0:T(1024)(128)(4,1)} %bitcast.102), calls=%async_computation.5 | async-start | bytes 8388608
  181.8 164.1 %all-to-all-start = ((bf16[16,128,224]{1,2,0:T(8,128)(2,1)}), bf16[16,128,224]{1,2,0:T(8,128)(2,1)S(1)}, u32[]{:S(2)}, u32[]{:S(2)}) async-start(bf16[16,128,224]{1,2,0:T(8,128)(2,1)} %bitcast.101), calls=%async_computation | async-start | bytes 1835008 | tf_op jit(solution)/shard_map/all_to_all | solution.py:303
  192.7 17.5 %copy-start.8 = (bf16[2048,224]{0,1:T(8,128)(2,1)S(1)}, bf16[2048,224]{0,1:T(8,128)(2,1)}, u32[]{:S(2)}) copy-start(bf16[2048,224]{0,1:T(8,128)(2,1)} %copy-done.7) | copy-start | bytes 2752516
  210.2 17.0 %copy-start.6 = (bf16[2048,224]{0,1:T(8,128)(2,1)S(1)}, bf16[2048,224]{0,1:T(8,128)(2,1)}, u32[]{:S(2)}) copy-start(bf16[2048,224]{0,1:T(8,128)(2,1)} %get-tuple-element.9) | copy-start | bytes 2752516
  336.4 5.9 %copy-start.3 = (f32[224,2048]{1,0:T(8,128)S(1)}, f32[224,2048]{1,0:T(8,128)}, u32[]{:S(2)}) copy-start(f32[224,2048]{1,0:T(8,128)} %fusion) | copy-start | bytes 5505028
  336.4 5.9 %copy-start.4 = (f32[224,2048]{1,0:T(8,128)S(1)}, f32[224,2048]{1,0:T(8,128)}, u32[]{:S(2)}) copy-start(f32[224,2048]{1,0:T(8,128)} %fusion.8) | copy-start | bytes 5505028
  336.4 5.9 %copy-start.5 = (f32[224,2048]{1,0:T(8,128)S(1)}, f32[224,2048]{1,0:T(8,128)}, u32[]{:S(2)}) copy-start(f32[224,2048]{1,0:T(8,128)} %fusion.2) | copy-start | bytes 5505028
  345.9 1.3 copy-start.1

commit v3 on v2

--- a/solution.py
+++ b/solution.py
@@ -43,7 +43,7 @@
     return to_a, to_b, to_z, to_core
 
 
-def gather_kernel(groups, cores, x_ref, out_ref, own_sem, *sems):
+def gather_kernel(groups, cores, x_ref, gc_ref, gs_ref, uc_ref, us_ref, out_ref, w_ref, own_sem, *sems):
     me, core, z, line = place(groups)
     a, b, sa, sb = bits(me, core % 2)
     rows = x_ref.shape[0]
@@ -81,6 +81,14 @@
     send(x_ref, me, a_send.at[0], a_recv.at[0], to_a)
     to_cores(x_ref, me, 0)
     own.start()
+
+    owned, blocks = gs_ref.shape
+    step = gc_ref.shape[1] // blocks
+    for first, codes, scales in ((0, gc_ref, gs_ref), (owned, uc_ref, us_ref)):
+        for blk in range(blocks):
+            values = codes[:, blk * step:(blk + 1) * step].astype(jnp.float32)
+            values = values * scales[:, blk:blk + 1]
+            w_ref[first:first + owned, blk * step:(blk + 1) * step] = values.astype(w_ref.dtype)
 
     def take_a(j):
         zz = lax.rem(z - j + line, line)
@@ -121,15 +129,20 @@
         copy.wait_send()
 
 
-def gather_tokens(tokens, groups, cores):
+def gather_tokens(tokens, gate_codes, gate_scales, up_codes, up_scales, groups, cores):
     rows, wide = tokens.shape
     line = groups // 4
     dma = pltpu.SemaphoreType.DMA
     return pl.pallas_call(
         functools.partial(gather_kernel, groups, cores),
-        out_shape=jax.ShapeDtypeStruct((cores, groups * rows, wide), tokens.dtype),
-        in_specs=[pl.BlockSpec(memory_space=pl.ANY)],
-        out_specs=pl.BlockSpec(memory_space=pl.ANY),
+        out_shape=(
+            jax.ShapeDtypeStruct((cores, groups * rows, wide), tokens.dtype),
+            jax.ShapeDtypeStruct((2 * gate_codes.shape[0], gate_codes.shape[1]), jnp.bfloat16),
+        ),
+        in_specs=[pl.BlockSpec(memory_space=pl.ANY)] + [pl.BlockSpec(memory_space=pltpu.VMEM)] * 4,
+        out_specs=(
+            pl.BlockSpec(memory_space=pl.ANY), pl.BlockSpec(memory_space=pltpu.VMEM),
+        ),
         scratch_shapes=[
             dma,
             dma((line - 1,)), dma((line - 1,)),
@@ -139,16 +152,21 @@
         ],
         compiler_params=pltpu.CompilerParams(collective_id=0, has_side_effects=True),
         name="gather_tokens",
-    )(tokens)
-
-
-def scatter_kernel(groups, cores, x_ref, out_ref, acc, from_core, from_a, from_b, from_z, *sems):
+    )(tokens, gate_codes, gate_scales, up_codes, up_scales)
+
+
+def scatter_kernel(groups, cores, d_ref, w_ref, h_ref, out_ref, hid_ref, sums, outbox,
+                   from_core, from_a, from_b, from_z, *sems):
     me, core, z, line = place(groups)
     a, b, sa, sb = bits(me, core % 2)
     rows, wide = out_ref.shape
     to_a, to_b, to_z, to_core = peers_of(me, core, z, line, cores, a, b, sa, sb)
-    greet([to_a, to_b] + to_z + to_core)
-    own_sem, c_send, c_recv, a_send, a_recv, b_send, b_recv, z_send, z_recv = sems
+    to_all = [{"inter": lax.rem(me + i, groups)} for i in range(1, groups)]
+    greet(to_all + to_core)
+    (c_send, c_recv, a_send, a_recv, b_send, b_recv, z_send, z_recv, h_send, h_recv,
+     h_own) = sems
+    ring = outbox.shape[0]
+    tile = min(512, wide)
 
     def block_at(parity, k, j):
         pa, pb, psa, psb = bits(me, parity)
@@ -156,13 +174,7 @@
         bb = 1 - pb if k % 2 == 0 else pb
         return block_of(lax.rem(z + 1 + j, line), aa, bb, psa, psb)
 
-    def part(block, slab):
-        return x_ref.at[
-            pl.ds(pl.multiple_of(block * rows, rows), rows),
-            pl.ds(pl.multiple_of(slab * wide, wide), wide),
-        ]
-
-    started, loads = [], {}
+    started = []
 
     def remote(src, dst, send_sem, recv_sem, peer):
         return pltpu.make_async_remote_copy(
@@ -175,110 +187,134 @@
         copy.start()
         started.append(copy)
 
-    for k in range(4):
-        for j in range(line):
-            slot = k * line + j
-            for i in range(1, cores):
-                other = lax.rem(core + i, cores)
-                block = block_at(other % 2, k, j)
-                send(part(block, other), from_core.at[i - 1, slot], c_send.at[i - 1, slot],
-                     c_recv.at[i - 1, slot], to_core[i - 1])
-            loads[slot] = pltpu.make_async_copy(
-                part(block_at(core % 2, k, j), core), acc.at[slot], own_sem.at[slot])
-            loads[slot].start()
-
-    def group_sum(slot, extras):
-        loads[slot].wait()
+    def add(block, slab, refs, dst):
+        here = pl.ds(pl.multiple_of(block * rows, rows), rows)
+
+        def body(t, _):
+            cols = pl.ds(pl.multiple_of(t * tile, tile), tile)
+            total = jnp.dot(
+                d_ref[here, :],
+                w_ref[:, pl.ds(pl.multiple_of(slab * wide + t * tile, tile), tile)],
+                preferred_element_type=jnp.float32,
+            )
+            for ref in refs:
+                total = total + ref[:, cols].astype(jnp.float32)
+            dst[:, cols] = total.astype(dst.dtype)
+            return 0
+
+        lax.fori_loop(0, wide // tile, body, 0)
+
+    pending = {}
+
+    def give(slot):
+        k, j = slot // line, slot % line
+        for i in range(1, cores):
+            other = lax.rem(core + i, cores)
+            box = outbox.at[slot % ring, i - 1]
+            if (slot % ring, i) in pending:
+                pending[slot % ring, i].wait_send()
+            add(block_at(other % 2, k, j), other, [], box)
+            copy = remote(box, from_core.at[i - 1, slot], c_send.at[i - 1, slot],
+                          c_recv.at[i - 1, slot], to_core[i - 1])
+            copy.start()
+            pending[slot % ring, i] = copy
+
+    def own(slot):
+        return block_at(core % 2, slot // line, slot % line)
+
+    def given(slot):
         for i in range(cores - 1):
-            remote(acc.at[slot], from_core.at[i, slot], c_send.at[i, slot], c_recv.at[i, slot],
+            remote(outbox.at[0, i], from_core.at[i, slot], c_send.at[i, slot], c_recv.at[i, slot],
                    to_core[i]).wait_recv()
-        refs = [acc.at[slot]] + [from_core.at[i, slot] for i in range(cores - 1)] + extras
-        return refs
-
-    def add(refs, dst):
-        step = 16
-
-        def body(r, _):
-            here = pl.ds(pl.multiple_of(r * step, step), step)
-            total = refs[0][here, :].astype(jnp.float32)
-            for ref in refs[1:]:
-                total = total + ref[here, :].astype(jnp.float32)
-            dst[here, :] = total.astype(dst.dtype)
-            return 0
-
-        lax.fori_loop(0, rows // step, body, 0)
-
+        return [from_core.at[i, slot] for i in range(cores - 1)]
+
+    def hidden_of(block):
+        return h_ref.at[pl.ds(pl.multiple_of(block * rows, rows), rows), :]
+
+    give(0)
+    give(1)
     for slot in range(2 * line):
-        add(group_sum(slot, []), acc.at[slot])
-        send(acc.at[slot], from_a.at[slot], a_send.at[slot], a_recv.at[slot], to_a)
+        for later in (2 * slot + 2, 2 * slot + 3):
+            if later < 4 * line:
+                give(later)
+        add(own(slot), core, given(slot), sums.at[slot])
+        send(sums.at[slot], from_a.at[slot], a_send.at[slot], a_recv.at[slot], to_a)
+    for i in range(1, groups):
+        peer = lax.rem(me + i, groups)
+        send(hidden_of(peer), hid_ref.at[me], h_send.at[i - 1], h_recv.at[i - 1], to_all[i - 1])
+    kept = pltpu.make_async_copy(hidden_of(me), hid_ref.at[me], h_own)
+    kept.start()
     for j in range(line):
         slot = 2 * line + j
-        refs = group_sum(slot, [from_a.at[j]])
-        remote(acc.at[slot], from_a.at[j], a_send.at[j], a_recv.at[j], to_a).wait_recv()
-        add(refs, acc.at[slot])
-        send(acc.at[slot], from_b.at[j], b_send.at[j], b_recv.at[j], to_b)
+        refs = given(slot) + [from_a.at[j]]
+        remote(sums.at[slot], from_a.at[j], a_send.at[j], a_recv.at[j], to_a).wait_recv()
+        add(own(slot), core, refs, sums.at[slot])
+        send(sums.at[slot], from_b.at[j], b_send.at[j], b_recv.at[j], to_b)
     for j in range(line):
         slot = 3 * line + j
-        refs = group_sum(slot, [from_a.at[line + j], from_b.at[j]])
-        remote(acc.at[slot], from_a.at[line + j], a_send.at[line + j], a_recv.at[line + j],
+        refs = given(slot) + [from_a.at[line + j], from_b.at[j]]
+        remote(sums.at[slot], from_a.at[line + j], a_send.at[line + j], a_recv.at[line + j],
                to_a).wait_recv()
-        remote(acc.at[slot], from_b.at[j], b_send.at[j], b_recv.at[j], to_b).wait_recv()
+        remote(sums.at[slot], from_b.at[j], b_send.at[j], b_recv.at[j], to_b).wait_recv()
         if j < line - 1:
-            add(refs, acc.at[slot])
-            send(acc.at[slot], from_z.at[j], z_send.at[j], z_recv.at[j], to_z[j])
+            add(own(slot), core, refs, sums.at[slot])
+            send(sums.at[slot], from_z.at[j], z_send.at[j], z_recv.at[j], to_z[j])
         else:
             for i in range(line - 1):
-                remote(acc.at[slot], from_z.at[i], z_send.at[i], z_recv.at[i], to_z[i]).wait_recv()
-            add(refs + [from_z.at[i] for i in range(line - 1)], out_ref)
-    for copy in started:
+                remote(sums.at[slot], from_z.at[i], z_send.at[i], z_recv.at[i], to_z[i]).wait_recv()
+            add(own(slot), core, refs + [from_z.at[i] for i in range(line - 1)], out_ref)
+    for i in range(1, groups):
+        peer = lax.rem(me - i + groups, groups)
+        remote(hidden_of(me), hid_ref.at[peer], h_send.at[i - 1], h_recv.at[i - 1],
+               to_all[i - 1]).wait_recv()
+    kept.wait()
+    for copy in started + list(pending.values()):
         copy.wait_send()
 
 
-def scatter_sum(partial_sum, groups, cores):
-    tokens, width = partial_sum.shape
+def scatter_sum(d_both, w_both, hidden, groups, cores):
+    tokens, width = d_both.shape[0], w_both.shape[1]
     rows, wide, line = tokens // groups, width // cores, groups // 4
     dma = pltpu.SemaphoreType.DMA
 
     def slots(*count):
-        return pltpu.VMEM((*count, rows, wide), partial_sum.dtype)
+        return pltpu.VMEM((*count, rows, wide), jnp.bfloat16)
 
     return pl.pallas_call(
         functools.partial(scatter_kernel, groups, cores),
-        out_shape=jax.ShapeDtypeStruct((rows, wide), partial_sum.dtype),
-        in_specs=[pl.BlockSpec(memory_space=pl.ANY)],
-        out_specs=pl.BlockSpec(memory_space=pltpu.VMEM),
+        out_shape=(
+            jax.ShapeDtypeStruct((rows, wide), jnp.bfloat16),
+            jax.ShapeDtypeStruct((groups, rows, hidden.shape[1]), hidden.dtype),
+        ),
+        in_specs=[
+            pl.BlockSpec(memory_space=pltpu.VMEM), pl.BlockSpec(memory_space=pltpu.VMEM),
+            pl.BlockSpec(memory_space=pl.ANY),
+        ],
+        out_specs=(
+            pl.BlockSpec(memory_space=pltpu.VMEM), pl.BlockSpec(memory_space=pl.ANY),
+        ),
         scratch_shapes=[
-            slots(4 * line), slots(cores - 1, 4 * line), slots(2 * line), slots(line),
-            slots(line - 1),
-            dma((4 * line,)),
+            slots(4 * line), slots(4, cores - 1), slots(cores - 1, 4 * line), slots(2 * line),
+            slots(line), slots(line - 1),
             dma((cores - 1, 4 * line)), dma((cores - 1, 4 * line)),
             dma((2 * line,)), dma((2 * line,)),
             dma((line,)), dma((line,)),
             dma((line - 1,)), dma((line - 1,)),
+            dma((groups - 1,)), dma((groups - 1,)), dma,
         ],
         compiler_params=pltpu.CompilerParams(collective_id=1, has_side_effects=True),
         name="scatter_sum",
-    )(partial_sum)
-
-
-def dequantize(codes, scales):
-    rows, width = codes.shape
-    blocks = scales.shape[1]
-    step = width // blocks
-    parts = [
-        codes[:, b * step:(b + 1) * step].astype(jnp.float32) * scales[:, b:b + 1]
-        for b in range(blocks)
-    ]
-    return jnp.concatenate(parts, axis=1).astype(jnp.bfloat16)
+    )(d_both, w_both, hidden)
 
 
 def per_device(tokens, gate_codes, gate_scales, up_codes, up_scales, cotangent):
     groups = lax.axis_size("inter")
-    whole = gather_tokens(tokens, groups, lax.axis_size("intra"))
+    whole, w_both = gather_tokens(
+        tokens, gate_codes, gate_scales, up_codes, up_scales, groups, lax.axis_size("intra")
+    )
     slabs, count, wide = whole.shape
     back = lax.all_to_all(cotangent, "inter", split_axis=1, concat_axis=0, tiled=True)
-    w_gate = dequantize(gate_codes, gate_scales)
-    w_up = dequantize(up_codes, up_scales)
+    owned = gate_codes.shape[0]
 
     def forward(weights):
         total = None
@@ -292,21 +328,18 @@
             total = term if total is None else total + term
         return total
 
-    gate = forward(w_gate)
-    up = forward(w_up)
+    gate = forward(w_both[:owned])
+    up = forward(w_both[owned:])
     sig = jax.nn.sigmoid(gate)
     act = gate * sig
     hidden = (act * up).astype(jnp.bfloat16)
     back = back.astype(jnp.float32)
     d_up = (back * act).astype(jnp.bfloat16)
     d_gate = (back * up * sig * (1.0 + gate * (1.0 - sig))).astype(jnp.bfloat16)
-    hidden = lax.all_to_all(hidden, "inter", split_axis=0, concat_axis=1, tiled=True)
-
-    partial_sum = jnp.dot(d_gate, w_gate, preferred_element_type=jnp.float32)
-    partial_sum = partial_sum + jnp.dot(d_up, w_up, preferred_element_type=jnp.float32)
-    token_grad = scatter_sum(
-        partial_sum.astype(jnp.bfloat16), groups, lax.axis_size("intra")
+    token_grad, parts = scatter_sum(
+        jnp.concatenate([d_gate, d_up], axis=1), w_both, hidden, groups, lax.axis_size("intra")
     )
+    hidden = parts.transpose(1, 0, 2).reshape(parts.shape[1], groups * owned)
 
     def rows_grad(d_rows):
         terms = [

time: 352 us -> 293 us (0.83)
  matrix products: 80.9 us -> 46.2 us
  other arithmetic: 36 us -> 8.81 us
  Pallas kernels: 207 us -> 219 us
  starting transfers between devices: 17.9 us -> 6.94 us
  local copies, waits for them, and re-layouts: 5.48 us -> 9.21 us
    dot_general x2 -> x0, matrix products: 34.5 us -> none  [the longest x1 17.5 us: per_device(): partial_sum = jnp.dot(d_gate, w_gate, preferred_element_type=jnp.float32)]
    unnamed x31 -> x2, other arithmetic: 30.4 us -> 0.01 us
    pallas_call x1, Pallas kernels: 102 us -> 114 us  [scatter_sum(): pl.pallas_call(functools.partial(scatter_kernel, groups, cores), out_shap...]
    all_to_all x1 -> x0, starting transfers between devices: 10.9 us -> none  [per_device(): lax.all_to_all(hidden, 'inter', split_axis=0, concat_axis=1, tiled=True)]
    dot_general x4, matrix products: 23.3 us -> 19.1 us  [rows_grad(): lax.dot_general(d_rows, whole[s], (((0,), (0,)), ((), ())), preferred_ele...]
    dot_general x4, matrix products: 23.1 us -> 27.1 us  [forward(): lax.dot_general(whole[s], weights[:, s * wide:(s + 1) * wide], (((1,), (1...]
  transfers between devices with their start and end apart: 2 -> 1, of which waited for: 0 -> 0; matrix products, arithmetic and copies ran while one was open for 28% -> 6% of each run, Pallas kernels for 59% -> 36%
where the time goes in v3:
time: 293 us; the launch traced here: 290 us
  Pallas kernels  219 us (75%)
  matrix products  46.2 us (16%)
  local copies, waits for them, and re-layouts  9.21 us (3%)
  other arithmetic  8.81 us (3%)
  starting transfers between devices  6.94 us (2%)
    pallas_call x1, Pallas kernels, scatter_sum(): pl.pallas_call(functools.partial(scatter_kernel, groups, cores), out_shap...  114 us
    pallas_call x1, Pallas kernels, gather_tokens(): pl.pallas_call(functools.partial(gather_kernel, groups, cores), out_shape...  105 us
    dot_general x4, matrix products, forward(): lax.dot_general(whole[s], weights[:, s * wide:(s + 1) * wide], (((1,), (1...  27.1 us
    dot_general x4, matrix products, rows_grad(): lax.dot_general(d_rows, whole[s], (((0,), (0,)), ((), ())), preferred_ele...  19.1 us
    all_to_all x1, starting transfers between devices, per_device(): lax.all_to_all(cotangent, 'inter', split_axis=1, concat_axis=0, tiled=True)  6.94 us
    div x1, other arithmetic, rows_grad(): return jnp.concatenate(terms, axis=1) / groups  6.5 us
  transfers between devices with their start and end apart: 1, of which 0 were waited for; matrix products, arithmetic and copies ran while one was open for 6% of the time, Pallas kernels for 36%

profile of v3, /device:TPU:28, one launch (start us, length us, event | category | flops | bytes accessed | tf_op | source)
XLA Modules:
  0.0 290.5 jit_solution(18397478132011107865)
XLA Ops:
  0.6 0.0 copy-start.2
  0.6 0.0 copy-start.3
  0.7 2.2 copy.17
  2.9 6.9 %all-to-all-start = ((bf16[128,16,224]{0,2,1:T(8,128)(2,1)}), bf16[128,16,224]{0,2,1:T(8,128)(2,1)S(1)}, u32[]{:S(2)}, u32[]{:S(2)}) async-start(bf16[128,16,224]{0,2,1:T(8,128)(2,1)} %bitcast), calls=%async_computation | async-start | bytes 1835008 | tf_op jit(solution)/shard_map/all_to_all | solution.py:316
  9.8 0.0 copy-done.2
  9.8 0.7 copy.19.gs_ref
  10.6 0.0 copy-done.3
  10.6 0.7 copy.20.us_ref
  11.3 104.6 %gather_tokens.1 = (bf16[2,2048,2048]{2,1,0:T(8,128)(2,1)}, bf16[448,4096]{1,0:T(8,128)(2,1)}) custom-call(bf16[128,2048]{1,0:T(8,128)(2,1)} %x_ref.1, bf16[224,4096]{1,0:T(8,128)(2,1)} %gc_ref.1, f32[224,16]{1,0:T(8,128)} %copy.19.gs_ref, bf16[224,4096]{1,0:T(8,128)(2,1)} %uc_ref.1, f32[224,16]{1,0:T(8,128)} %copy.20.us_ref), custom_call_target="tpu_custom_call" | custom-call | tf_op jit(solution)/shard_map/gather_tokens/pallas_call | solution.py:136
  115.9 0.0 copy-start
  115.9 0.0 slice-start
  115.9 0.0 slice-start.1
  115.9 6.2 %fusion.4 = f32[2048,224]{1,0:T(8,128)S(1)} fusion(bf16[2,2048,2048]{2,1,0:T(8,128)(2,1)} %get-tuple-element.8, bf16[448,4096]{1,0:T(8,128)(2,1)} %get-tuple-element.9.w_ref), kind=kOutput, calls=%fused_computation.4 | convolution fusion | flops 1879048192 | bytes 11141120 | tf_op jit(solution)/shard_map/dot_general | solution.py:322
  122.1 0.0 copy-done
  122.1 0.0 slice-start.2
  122.2 0.0 slice-start.3
  122.2 7.2 %fusion.6 = f32[2048,224]{1,0:T(8,128)} fusion(bf16[2,2048,2048]{2,1,0:T(8,128)(2,1)} %get-tuple-element.8, bf16[448,4096]{1,0:T(8,128)(2,1)S(1)} %copy-done), kind=kOutput, calls=%fused_computation.6 | convolution fusion | flops 1879048192 | bytes 11141120 | tf_op jit(solution)/shard_map/dot_general | solution.py:322
  129.4 0.0 slice-done
  129.4 0.0 slice-done.1
  129.4 0.0 slice-done.2
  129.4 0.0 slice-done.3
  129.4 3.9 %fusion.27 = f32[2048,224]{1,0:T(8,128)} fusion(f32[2048,224]{1,0:T(8,128)S(1)} %fusion.4, bf16[2,2048,2048]{2,1,0:T(8,128)(2,1)S(1)} %bitcast.47, bf16[448,4096]{1,0:T(8,128)(2,1)S(1)} %copy-done), kind=kOutput, calls=%fused_computation.27 | convolution fusion | flops 1879506944 | bytes 13238272 | tf_op jit(solution)/shard_map/dot_general | solution.py:322
  133.3 0.0 all-to-all-done
  133.3 0.2 convert_bitcast_fusion
  133.5 1.8 copy.18
  135.3 9.8 %multiply_convert_fusion = (bf16[2048,224]{1,0:T(8,128)(2,1)}, bf16[2048,224]{1,0:T(8,128)(2,1)S(1)}, bf16[2048,224]{1,0:T(8,128)(2,1)S(1)}) fusion(f32[2048,224]{1,0:T(8,128)} %fusion.27, f32[16,128,224]{2,1,0:T(8,128)} %copy.18, f32[2048,224]{1,0:T(8,128)} %fusion.6, bf16[448,4096]{1,0:T(8,128)(2,1)} %get-tuple-element.9.w_ref, ...), kind=kOutput, calls=%fused_computation.35 | convolution fusion | flops 1886388224 | bytes 18350080 | tf_op jit(solution)/shard_map/dot_general | solution.py:322
  145.1 0.0 slice-start.4
  145.1 0.0 slice-start.5
  145.1 5.6 %fusion.2 = f32[224,2048]{1,0:T(8,128)S(1)} fusion(bf16[2048,224]{1,0:T(8,128)(2,1)S(1)} %get-tuple-element.17, bf16[2,2048,2048]{2,1,0:T(8,128)(2,1)} %get-tuple-element.8), kind=kOutput, calls=%fused_computation.2 | convolution fusion | flops 1879048192 | bytes 11141120 | tf_op jit(solution)/shard_map/dot_general | solution.py:346
  150.7 0.0 slice-start.6
  150.7 0.0 slice-start.7
  150.7 6.9 %fusion.10 = f32[224,2048]{1,0:T(8,128)} fusion(bf16[2048,224]{1,0:T(8,128)(2,1)S(1)} %get-tuple-element.17, bf16[2,2048,2048]{2,1,0:T(8,128)(2,1)} %get-tuple-element.8), kind=kOutput, calls=%fused_computation.10 | convolution fusion | flops 1879048192 | bytes 11141120 | tf_op jit(solution)/shard_map/dot_general | solution.py:346
  157.6 2.1 pad_maximum_fusion.d_ref
  159.7 0.0 slice-done.4
  159.7 0.0 slice-done.5
  159.7 0.0 slice-done.6
  159.7 0.0 slice-done.7
  159.7 3.3 %fusion = f32[224,2048]{1,0:T(8,128)} fusion(bf16[2048,224]{1,0:T(8,128)(2,1)S(1)} %get-tuple-element.18, bf16[2,2048,2048]{2,1,0:T(8,128)(2,1)S(1)} %bitcast.49), kind=kOutput, calls=%fused_computation | convolution fusion | flops 1879048192 | bytes 11272192 | tf_op jit(solution)/shard_map/dot_general | solution.py:346
  163.1 3.3 %fusion.8 = f32[224,2048]{1,0:T(8,128)} fusion(bf16[2048,224]{1,0:T(8,128)(2,1)S(1)} %get-tuple-element.18, bf16[2,2048,2048]{2,1,0:T(8,128)(2,1)S(1)} %bitcast.49), kind=kOutput, calls=%fused_computation.8 | convolution fusion | flops 1879048192 | bytes 11272192 | tf_op jit(solution)/shard_map/dot_general | solution.py:346
  166.4 113.9 %scatter_sum.1 = (bf16[128,2048]{1,0:T(8,128)(2,1)}, bf16[16,128,224]{2,1,0:T(8,128)(2,1)}) custom-call(bf16[2048,448]{1,0:T(8,128)(2,1)} %pad_maximum_fusion.d_ref, bf16[448,4096]{1,0:T(8,128)(2,1)} %get-tuple-element.9.w_ref, bf16[2048,224]{1,0:T(8,128)(2,1)} %get-tuple-element.16.h_ref), custom_call_target="tpu_custom_call" | custom-call | tf_op jit(solution)/shard_map/scatter_sum/pallas_call | solution.py:283
  280.3 1.6 copy.25
  281.9 1.3 copy.26
  283.2 0.0 copy-start.1
  283.2 6.5 %maximum_multiply_fusion = (f32[224,4096]{1,0:T(8,128)}, f32[224,4096]{1,0:T(8,128)}) fusion(f32[224,2048]{1,0:T(8,128)S(1)} %fusion.2, f32[224,2048]{1,0:T(8,128)} %fusion.10, f32[224,2048]{1,0:T(8,128)} %fusion, f32[224,2048]{1,0:T(8,128)} %fusion.8), kind=kLoop, calls=%fused_computation.24 | loop fusion | flops 3670016 | bytes 14680064 | tf_op jit(solution)/shard_map/div | solution.py:351
  289.7 0.0 copy-done.1
  289.7 0.8 copy.32
  (2 shorter events, 0.0 us)
Async XLA Ops:
  0.6 9.2 %copy-start.2 = (f32[224,16]{0,1:T(8,128)S(1)}, f32[224,16]{0,1:T(8,128)}, u32[]{:S(2)}) copy-start(f32[224,16]{0,1:T(8,128)} %param.8) | copy-start | bytes 43012
  0.6 9.9 %copy-start.3 = (f32[224,16]{0,1:T(8,128)S(1)}, f32[224,16]{0,1:T(8,128)}, u32[]{:S(2)}) copy-start(f32[224,16]{0,1:T(8,128)} %param.10) | copy-start | bytes 43012
  2.9 130.4 %all-to-all-start = ((bf16[128,16,224]{0,2,1:T(8,128)(2,1)}), bf16[128,16,224]{0,2,1:T(8,128)(2,1)S(1)}, u32[]{:S(2)}, u32[]{:S(2)}) async-start(bf16[128,16,224]{0,2,1:T(8,128)(2,1)} %bitcast), calls=%async_computation | async-start | bytes 1835008 | tf_op jit(solution)/shard_map/all_to_all | solution.py:316
  115.9 6.3 %copy-start = (bf16[448,4096]{1,0:T(8,128)(2,1)S(1)}, bf16[448,4096]{1,0:T(8,128)(2,1)}, u32[]{:S(2)}) copy-start(bf16[448,4096]{1,0:T(8,128)(2,1)} %get-tuple-element.9.w_ref) | copy-start | bytes 11010052
  115.9 13.5 %slice-start = ((s8[16777216]{0:T(1024)(128)(4,1)}), s8[4194304]{0:T(1024)(128)(4,1)S(1)}, s32[]{:S(2)}) async-start(s8[16777216]{0:T(1024)(128)(4,1)} %bitcast.46), calls=%async_computation.1 | async-start | bytes 8388608
  115.9 13.5 %slice-start.1 = ((s8[16777216]{0:T(1024)(128)(4,1)}), s8[4194304]{0:T(1024)(128)(4,1)S(1)}, s32[]{:S(2)}) async-start(s8[16777216]{0:T(1024)(128)(4,1)} %bitcast.46), calls=%async_computation.2 | async-start | bytes 8388608
  122.1 7.3 %slice-start.2 = ((s8[16777216]{0:T(1024)(128)(4,1)}), s8[4194304]{0:T(1024)(128)(4,1)S(1)}, s32[]{:S(2)}) async-start(s8[16777216]{0:T(1024)(128)(4,1)} %bitcast.46), calls=%async_computation.3 | async-start | bytes 8388608
  122.2 7.3 %slice-start.3 = ((s8[16777216]{0:T(1024)(128)(4,1)}), s8[4194304]{0:T(1024)(128)(4,1)S(1)}, s32[]{:S(2)}) async-start(s8[16777216]{0:T(1024)(128)(4,1)} %bitcast.46), calls=%async_computation.4 | async-start | bytes 8388608
  145.1 14.6 %slice-start.4 = ((s8[16777216]{0:T(1024)(128)(4,1)}), s8[4194304]{0:T(1024)(128)(4,1)S(1)}, s32[]{:S(2)}) async-start(s8[16777216]{0:T(1024)(128)(4,1)} %bitcast.48), calls=%async_computation.5 | async-start | bytes 8388608
  145.1 14.6 %slice-start.5 = ((s8[16777216]{0:T(1024)(128)(4,1)}), s8[4194304]{0:T(1024)(128)(4,1)S(1)}, s32[]{:S(2)}) async-start(s8[16777216]{0:T(1024)(128)(4,1)} %bitcast.48), calls=%async_computation.6 | async-start | bytes 8388608
  150.7 9.0 %slice-start.6 = ((s8[16777216]{0:T(1024)(128)(4,1)}), s8[4194304]{0:T(1024)(128)(4,1)S(1)}, s32[]{:S(2)}) async-start(s8[16777216]{0:T(1024)(128)(4,1)} %bitcast.48), calls=%async_computation.7 | async-start | bytes 8388608
  150.7 9.0 %slice-start.7 = ((s8[16777216]{0:T(1024)(128)(4,1)}), s8[4194304]{0:T(1024)(128)(4,1)S(1)}, s32[]{:S(2)}) async-start(s8[16777216]{0:T(1024)(128)(4,1)} %bitcast.48), calls=%async_computation.8 | async-start | bytes 8388608
  283.2 6.5 %copy-start.1 = (bf16[128,2048]{1,0:T(8,128)(2,1)S(1)}, bf16[128,2048]{1,0:T(8,128)(2,1)}, u32[]{:S(2)}) copy-start(bf16[128,2048]{1,0:T(8,128)(2,1)} %get-tuple-element.26) | copy-start | bytes 1572868

commit v4 on v3

--- a/solution.py
+++ b/solution.py
@@ -49,37 +49,55 @@
     rows = x_ref.shape[0]
     to_a, to_b, to_z, to_core = peers_of(me, core, z, line, cores, a, b, sa, sb)
     greet([to_a, to_b] + to_z + to_core)
-    z_send, z_recv, b_send, b_recv, a_send, a_recv, c_send, c_recv = sems
+    up_send, down_send, z_recv, b_send, b_recv, a_send, a_recv, c_send, c_recv = sems
 
     def at(slab, block):
         return out_ref.at[slab, pl.ds(pl.multiple_of(block * rows, rows), rows), :]
 
-    started = []
-
-    def send(src, block, send_sem, recv_sem, peer):
-        copy = pltpu.make_async_remote_copy(
-            src_ref=src, dst_ref=at(core, block), send_sem=send_sem, recv_sem=recv_sem,
+    def copy_of(src, slab, block, send_sem, recv_sem, peer):
+        return pltpu.make_async_remote_copy(
+            src_ref=src, dst_ref=at(slab, block), send_sem=send_sem, recv_sem=recv_sem,
             device_id=peer, device_id_type=MESH,
         )
-        copy.start()
-        started.append(copy)
-
-    def arrived(slab, block, send_sem, recv_sem, peer):
-        pltpu.make_async_remote_copy(
-            src_ref=x_ref, dst_ref=at(slab, block), send_sem=send_sem, recv_sem=recv_sem,
-            device_id=peer, device_id_type=MESH,
-        ).wait_recv()
-
-    def to_cores(src, block, slot):
-        for i, peer in enumerate(to_core):
-            send(src, block, c_send.at[i, slot], c_recv.at[i, slot], peer)
+
+    def block(k, zz, parity=None):
+        pa, pb, psa, psb = bits(me, core % 2 if parity is None else parity)
+        return block_of(zz, 1 - pa if k >= 2 else pa, 1 - pb if k % 2 else pb, psa, psb)
+
+    up = {"inter": block_of(lax.rem(z + 1, line), a, b, sa, sb)}
+    down = {"inter": block_of(lax.rem(z - 1 + line, line), a, b, sa, sb)}
+
+    def to_a_copy(src, k, zz):
+        return copy_of(src, core, block(k, zz), a_send.at[k, zz], a_recv.at[k, zz], to_a)
+
+    def to_b_copy(src, zz):
+        return copy_of(src, core, block(0, zz), b_send.at[zz], b_recv.at[zz], to_b)
+
+    def core_copies(src, k, zz):
+        return [
+            copy_of(src, core, block(k, zz), c_send.at[i, k, zz], c_recv.at[i, k, zz], peer)
+            for i, peer in enumerate(to_core)
+        ]
+
+    def line_copy(src, zz, upward):
+        sems_of, peer = (up_send, up) if upward else (down_send, down)
+        return copy_of(src, core, block(0, zz), sems_of.at[zz], z_recv.at[zz], peer)
+
+    def begin(copies):
+        for copy in copies:
+            copy.start()
 
     own = pltpu.make_async_copy(x_ref, at(core, me), own_sem)
-    for j in range(1, line):
-        send(x_ref, me, z_send.at[j - 1], z_recv.at[j - 1], to_z[j - 1])
-    send(x_ref, me, b_send.at[0], b_recv.at[0], to_b)
-    send(x_ref, me, a_send.at[0], a_recv.at[0], to_a)
-    to_cores(x_ref, me, 0)
+
+    @pl.when(z < line - 1)
+    def _():
+        line_copy(x_ref, z, True).start()
+
+    @pl.when(z > 0)
+    def _():
+        line_copy(x_ref, z, False).start()
+
+    begin([to_b_copy(x_ref, z), to_a_copy(x_ref, 0, z)] + core_copies(x_ref, 0, z))
     own.start()
 
     owned, blocks = gs_ref.shape
@@ -90,43 +108,71 @@
             values = values * scales[:, blk:blk + 1]
             w_ref[first:first + owned, blk * step:(blk + 1) * step] = values.astype(w_ref.dtype)
 
-    def take_a(j):
-        zz = lax.rem(z - j + line, line)
-        for k, bb in ((2, b), (3, 1 - b)):
-            block = block_of(zz, 1 - a, bb, sa, sb)
-            slot = (k - 2) * line + j
-            arrived(core, block, a_send.at[slot], a_recv.at[slot], to_a)
-            to_cores(at(core, block), block, k * line + j)
-
-    for j in range(line):
-        zz = lax.rem(z - j + line, line)
-        if j > 0:
-            block = block_of(zz, a, b, sa, sb)
-            arrived(core, block, z_send.at[j - 1], z_recv.at[j - 1], to_z[j - 1])
-            send(at(core, block), block, b_send.at[j], b_recv.at[j], to_b)
-            send(at(core, block), block, a_send.at[j], a_recv.at[j], to_a)
-            to_cores(at(core, block), block, j)
-        block = block_of(zz, a, 1 - b, sa, sb)
-        arrived(core, block, b_send.at[j], b_recv.at[j], to_b)
-        send(at(core, block), block, a_send.at[line + j], a_recv.at[line + j], to_a)
-        to_cores(at(core, block), block, line + j)
-        if j > 0:
-            take_a(j - 1)
-    take_a(line - 1)
+    def take_b(zz):
+        src = at(core, block(1, zz))
+        copy_of(x_ref, core, block(1, zz), b_send.at[zz], b_recv.at[zz], to_b).wait_recv()
+        begin([to_a_copy(src, 1, zz)] + core_copies(src, 1, zz))
+
+    def take_a(zz):
+        for k in (2, 3):
+            src = at(core, block(k, zz))
+            copy_of(x_ref, core, block(k, zz), a_send.at[k - 2, zz], a_recv.at[k - 2, zz],
+                    to_a).wait_recv()
+            begin(core_copies(src, k, zz))
+
+    def take_line(zz, upward):
+        src = at(core, block(0, zz))
+        line_copy(x_ref, zz, upward).wait_recv()
+
+        @pl.when(z < line - 1 if upward else z > 0)
+        def _():
+            line_copy(src, zz, upward).start()
+
+        begin([to_b_copy(src, zz), to_a_copy(src, 0, zz)] + core_copies(src, 0, zz))
+
+    def nearby(shift, act):
+        @pl.when(z >= shift)
+        def _():
+            act(z - shift, True)
+
+        @pl.when(z + shift < line)
+        def _():
+            act(z + shift, False)
+
+    take_b(z)
+    for shift in range(1, line):
+        nearby(shift, take_line)
+        if shift == 1:
+            take_a(z)
+        else:
+            nearby(shift - 1, lambda zz, _: take_a(zz))
+        nearby(shift, lambda zz, _: take_b(zz))
+    if line == 1:
+        take_a(z)
+    else:
+        nearby(line - 1, lambda zz, _: take_a(zz))
     for i in range(1, cores):
         other = lax.rem(core - i + cores, cores)
-        oa, ob, osa, osb = bits(me, other % 2)
-        for k, (da, db) in enumerate(((0, 0), (0, 1), (1, 0), (1, 1))):
-            aa = oa + da - 2 * da * oa
-            bb = ob + db - 2 * db * ob
-            for j in range(line):
-                zz = lax.rem(z - j + line, line)
-                block = block_of(zz, aa, bb, osa, osb)
-                slot = k * line + j
-                arrived(other, block, c_send.at[i - 1, slot], c_recv.at[i - 1, slot], to_core[i - 1])
+        for k in range(4):
+            for zz in range(line):
+                copy_of(x_ref, other, block(k, zz, other % 2), c_send.at[i - 1, k, zz],
+                        c_recv.at[i - 1, k, zz], to_core[i - 1]).wait_recv()
     own.wait()
-    for copy in started:
-        copy.wait_send()
+    for zz in range(line):
+        to_b_copy(x_ref, zz).wait_send()
+        for k in range(2):
+            to_a_copy(x_ref, k, zz).wait_send()
+        for k in range(4):
+            for copy in core_copies(x_ref, k, zz):
+                copy.wait_send()
+
+        @pl.when((zz <= z) & (z < line - 1))
+        def _():
+            line_copy(x_ref, zz, True).wait_send()
+
+        @pl.when((zz >= z) & (z > 0))
+        def _():
+            line_copy(x_ref, zz, False).wait_send()
 
 
 def gather_tokens(tokens, gate_codes, gate_scales, up_codes, up_scales, groups, cores):
@@ -145,10 +191,10 @@
         ),
         scratch_shapes=[
             dma,
-            dma((line - 1,)), dma((line - 1,)),
+            dma((line,)), dma((line,)), dma((line,)),
             dma((line,)), dma((line,)),
-            dma((2 * line,)), dma((2 * line,)),
-            dma((cores - 1, 4 * line)), dma((cores - 1, 4 * line)),
+            dma((2, line)), dma((2, line)),
+            dma((cores - 1, 4, line)), dma((cores - 1, 4, line)),
         ],
         compiler_params=pltpu.CompilerParams(collective_id=0, has_side_effects=True),
         name="gather_tokens",
@@ -206,18 +252,18 @@
 
     pending = {}
 
-    def give(slot):
+    def give(slot, n):
         k, j = slot // line, slot % line
         for i in range(1, cores):
             other = lax.rem(core + i, cores)
-            box = outbox.at[slot % ring, i - 1]
-            if (slot % ring, i) in pending:
-                pending[slot % ring, i].wait_send()
+            box = outbox.at[n % ring, i - 1]
+            if (n % ring, i) in pending:
+                pending[n % ring, i].wait_send()
             add(block_at(other % 2, k, j), other, [], box)
             copy = remote(box, from_core.at[i - 1, slot], c_send.at[i - 1, slot],
                           c_recv.at[i - 1, slot], to_core[i - 1])
             copy.start()
-            pending[slot % ring, i] = copy
+            pending[n % ring, i] = copy
 
     def own(slot):
         return block_at(core % 2, slot // line, slot % line)
@@ -231,38 +277,60 @@
     def hidden_of(block):
         return h_ref.at[pl.ds(pl.multiple_of(block * rows, rows), rows), :]
 
-    give(0)
-    give(1)
-    for slot in range(2 * line):
-        for later in (2 * slot + 2, 2 * slot + 3):
-            if later < 4 * line:
-                give(later)
-        add(own(slot), core, given(slot), sums.at[slot])
-        send(sums.at[slot], from_a.at[slot], a_send.at[slot], a_recv.at[slot], to_a)
-    for i in range(1, groups):
-        peer = lax.rem(me + i, groups)
-        send(hidden_of(peer), hid_ref.at[me], h_send.at[i - 1], h_recv.at[i - 1], to_all[i - 1])
-    kept = pltpu.make_async_copy(hidden_of(me), hid_ref.at[me], h_own)
-    kept.start()
-    for j in range(line):
-        slot = 2 * line + j
-        refs = given(slot) + [from_a.at[j]]
-        remote(sums.at[slot], from_a.at[j], a_send.at[j], a_recv.at[j], to_a).wait_recv()
-        add(own(slot), core, refs, sums.at[slot])
-        send(sums.at[slot], from_b.at[j], b_send.at[j], b_recv.at[j], to_b)
-    for j in range(line):
-        slot = 3 * line + j
-        refs = given(slot) + [from_a.at[line + j], from_b.at[j]]
-        remote(sums.at[slot], from_a.at[line + j], a_send.at[line + j], a_recv.at[line + j],
-               to_a).wait_recv()
-        remote(sums.at[slot], from_b.at[j], b_send.at[j], b_recv.at[j], to_b).wait_recv()
-        if j < line - 1:
+    order = []
+    for t in range(line + 2):
+        if t < line:
+            order += [(0, t), (1, t)]
+        if 0 <= t - 1 < line:
+            order.append((2, t - 1))
+        if 0 <= t - 2 < line:
+            order.append((3, t - 2))
+    order = [k * line + j for k, j in order]
+    ahead = iter(range(4 * line))
+
+    def give_next(count):
+        for n in ahead:
+            give(order[n], n)
+            count -= 1
+            if count == 0:
+                break
+
+    def take(ref, send_sem, recv_sem, peer):
+        remote(sums.at[0], ref, send_sem, recv_sem, peer).wait_recv()
+        return ref
+
+    def take_a(n):
+        return take(from_a.at[n], a_send.at[n], a_recv.at[n], to_a)
+
+    give_next(2)
+    for at, slot in enumerate(order):
+        give_next(2)
+        k, j = slot // line, slot % line
+        refs = given(slot)
+        if k < 2:
             add(own(slot), core, refs, sums.at[slot])
-            send(sums.at[slot], from_z.at[j], z_send.at[j], z_recv.at[j], to_z[j])
+            send(sums.at[slot], from_a.at[slot], a_send.at[slot], a_recv.at[slot], to_a)
+        elif k == 2:
+            refs.append(take_a(j))
+            add(own(slot), core, refs, sums.at[slot])
+            send(sums.at[slot], from_b.at[j], b_send.at[j], b_recv.at[j], to_b)
         else:
-            for i in range(line - 1):
-                remote(sums.at[slot], from_z.at[i], z_send.at[i], z_recv.at[i], to_z[i]).wait_recv()
-            add(own(slot), core, refs + [from_z.at[i] for i in range(line - 1)], out_ref)
+            refs.append(take_a(line + j))
+            refs.append(take(from_b.at[j], b_send.at[j], b_recv.at[j], to_b))
+            if j < line - 1:
+                add(own(slot), core, refs, sums.at[slot])
+                send(sums.at[slot], from_z.at[j], z_send.at[j], z_recv.at[j], to_z[j])
+            else:
+                for i in range(line - 1):
+                    refs.append(take(from_z.at[i], z_send.at[i], z_recv.at[i], to_z[i]))
+                add(own(slot), core, refs, out_ref)
+        if at == 2 * line - 1:
+            for i in range(1, groups):
+                peer = lax.rem(me + i, groups)
+                send(hidden_of(peer), hid_ref.at[me], h_send.at[i - 1], h_recv.at[i - 1],
+                     to_all[i - 1])
+            kept = pltpu.make_async_copy(hidden_of(me), hid_ref.at[me], h_own)
+            kept.start()
     for i in range(1, groups):
         peer = lax.rem(me - i + groups, groups)
         remote(hidden_of(me), hid_ref.at[peer], h_send.at[i - 1], h_recv.at[i - 1],

time: 293 us -> 270 us (0.922)
  Pallas kernels: 219 us -> 195 us
    pallas_call x1, Pallas kernels: 105 us -> 86.2 us  [gather_tokens(): pl.pallas_call(functools.partial(gather_kernel, groups, cores), out_shape...]
    pallas_call x1, Pallas kernels: 114 us -> 109 us  [scatter_sum(): pl.pallas_call(functools.partial(scatter_kernel, groups, cores), out_shap...]
  transfers between devices with their start and end apart: 1 -> 1, of which waited for: 0 -> 0; matrix products, arithmetic and copies ran while one was open for 6% -> 7% of each run, Pallas kernels for 36% -> 32%
where the time goes in v4:
time: 270 us; the launch traced here: 267 us
  Pallas kernels  195 us (72%)
  matrix products  46.2 us (17%)
  local copies, waits for them, and re-layouts  9.21 us (3%)
  other arithmetic  8.81 us (3%)
  starting transfers between devices  6.94 us (3%)
    pallas_call x1, Pallas kernels, scatter_sum(): pl.pallas_call(functools.partial(scatter_kernel, groups, cores), out_shap...  109 us
    pallas_call x1, Pallas kernels, gather_tokens(): pl.pallas_call(functools.partial(gather_kernel, groups, cores), out_shape...  86.2 us
    dot_general x4, matrix products, forward(): lax.dot_general(whole[s], weights[:, s * wide:(s + 1) * wide], (((1,), (1...  27.1 us
    dot_general x4, matrix products, rows_grad(): lax.dot_general(d_rows, whole[s], (((0,), (0,)), ((), ())), preferred_ele...  19.1 us
    all_to_all x1, starting transfers between devices, per_device(): lax.all_to_all(cotangent, 'inter', split_axis=1, concat_axis=0, tiled=True)  6.94 us
    div x1, other arithmetic, rows_grad(): return jnp.concatenate(terms, axis=1) / groups  6.5 us
    unnamed x29, local copies, waits for them, and re-layouts  5.83 us
  transfers between devices with their start and end apart: 1, of which 0 were waited for; matrix products, arithmetic and copies ran while one was open for 7% of the time, Pallas kernels for 32%

profile of v4, /device:TPU:28, one launch (start us, length us, event | category | flops | bytes accessed | tf_op | source)
XLA Modules:
  0.0 267.3 jit_solution(11943813045734748159)
XLA Ops:
  0.6 0.0 copy-start.2
  0.6 0.0 copy-start.3
  0.7 2.2 copy.17
  2.9 6.9 %all-to-all-start = ((bf16[128,16,224]{0,2,1:T(8,128)(2,1)}), bf16[128,16,224]{0,2,1:T(8,128)(2,1)S(1)}, u32[]{:S(2)}, u32[]{:S(2)}) async-start(bf16[128,16,224]{0,2,1:T(8,128)(2,1)} %bitcast), calls=%async_computation | async-start | bytes 1835008 | tf_op jit(solution)/shard_map/all_to_all | solution.py:384
  9.8 0.0 copy-done.2
  9.8 0.7 copy.19.gs_ref
  10.6 0.0 copy-done.3
  10.6 0.7 copy.20.us_ref
  11.3 86.2 %gather_tokens.1 = (bf16[2,2048,2048]{2,1,0:T(8,128)(2,1)}, bf16[448,4096]{1,0:T(8,128)(2,1)}) custom-call(bf16[128,2048]{1,0:T(8,128)(2,1)} %x_ref.1, bf16[224,4096]{1,0:T(8,128)(2,1)} %gc_ref.1, f32[224,16]{1,0:T(8,128)} %copy.19.gs_ref, bf16[224,4096]{1,0:T(8,128)(2,1)} %uc_ref.1, f32[224,16]{1,0:T(8,128)} %copy.20.us_ref), custom_call_target="tpu_custom_call" | custom-call | tf_op jit(solution)/shard_map/gather_tokens/pallas_call | solution.py:182
  97.5 0.0 copy-start
  97.6 0.0 slice-start
  97.6 0.0 slice-start.1
  97.6 6.2 %fusion.4 = f32[2048,224]{1,0:T(8,128)S(1)} fusion(bf16[2,2048,2048]{2,1,0:T(8,128)(2,1)} %get-tuple-element.8, bf16[448,4096]{1,0:T(8,128)(2,1)} %get-tuple-element.9.w_ref), kind=kOutput, calls=%fused_computation.4 | convolution fusion | flops 1879048192 | bytes 11141120 | tf_op jit(solution)/shard_map/dot_general | solution.py:390
  103.8 0.0 copy-done
  103.8 0.0 slice-start.2
  103.8 0.0 slice-start.3
  103.8 7.2 %fusion.6 = f32[2048,224]{1,0:T(8,128)} fusion(bf16[2,2048,2048]{2,1,0:T(8,128)(2,1)} %get-tuple-element.8, bf16[448,4096]{1,0:T(8,128)(2,1)S(1)} %copy-done), kind=kOutput, calls=%fused_computation.6 | convolution fusion | flops 1879048192 | bytes 11141120 | tf_op jit(solution)/shard_map/dot_general | solution.py:390
  111.1 0.0 slice-done
  111.1 0.0 slice-done.1
  111.1 0.0 slice-done.2
  111.1 0.0 slice-done.3
  111.1 3.9 %fusion.27 = f32[2048,224]{1,0:T(8,128)} fusion(f32[2048,224]{1,0:T(8,128)S(1)} %fusion.4, bf16[2,2048,2048]{2,1,0:T(8,128)(2,1)S(1)} %bitcast.47, bf16[448,4096]{1,0:T(8,128)(2,1)S(1)} %copy-done), kind=kOutput, calls=%fused_computation.27 | convolution fusion | flops 1879506944 | bytes 13238272 | tf_op jit(solution)/shard_map/dot_general | solution.py:390
  115.0 0.0 all-to-all-done
  115.0 0.2 convert_bitcast_fusion
  115.1 1.8 copy.18
  116.9 9.8 %multiply_convert_fusion = (bf16[2048,224]{1,0:T(8,128)(2,1)}, bf16[2048,224]{1,0:T(8,128)(2,1)S(1)}, bf16[2048,224]{1,0:T(8,128)(2,1)S(1)}) fusion(f32[2048,224]{1,0:T(8,128)} %fusion.27, f32[16,128,224]{2,1,0:T(8,128)} %copy.18, f32[2048,224]{1,0:T(8,128)} %fusion.6, bf16[448,4096]{1,0:T(8,128)(2,1)} %get-tuple-element.9.w_ref, ...), kind=kOutput, calls=%fused_computation.35 | convolution fusion | flops 1886388224 | bytes 18350080 | tf_op jit(solution)/shard_map/dot_general | solution.py:390
  126.7 0.0 slice-start.4
  126.7 0.0 slice-start.5
  126.7 5.6 %fusion.2 = f32[224,2048]{1,0:T(8,128)S(1)} fusion(bf16[2048,224]{1,0:T(8,128)(2,1)S(1)} %get-tuple-element.17, bf16[2,2048,2048]{2,1,0:T(8,128)(2,1)} %get-tuple-element.8), kind=kOutput, calls=%fused_computation.2 | convolution fusion | flops 1879048192 | bytes 11141120 | tf_op jit(solution)/shard_map/dot_general | solution.py:414
  132.3 0.0 slice-start.6
  132.3 0.0 slice-start.7
  132.3 6.9 %fusion.10 = f32[224,2048]{1,0:T(8,128)} fusion(bf16[2048,224]{1,0:T(8,128)(2,1)S(1)} %get-tuple-element.17, bf16[2,2048,2048]{2,1,0:T(8,128)(2,1)} %get-tuple-element.8), kind=kOutput, calls=%fused_computation.10 | convolution fusion | flops 1879048192 | bytes 11141120 | tf_op jit(solution)/shard_map/dot_general | solution.py:414
  139.2 2.1 pad_maximum_fusion.d_ref
  141.4 0.0 slice-done.4
  141.4 0.0 slice-done.5
  141.4 0.0 slice-done.6
  141.4 0.0 slice-done.7
  141.4 3.3 %fusion = f32[224,2048]{1,0:T(8,128)} fusion(bf16[2048,224]{1,0:T(8,128)(2,1)S(1)} %get-tuple-element.18, bf16[2,2048,2048]{2,1,0:T(8,128)(2,1)S(1)} %bitcast.49), kind=kOutput, calls=%fused_computation | convolution fusion | flops 1879048192 | bytes 11272192 | tf_op jit(solution)/shard_map/dot_general | solution.py:414
  144.7 3.3 %fusion.8 = f32[224,2048]{1,0:T(8,128)} fusion(bf16[2048,224]{1,0:T(8,128)(2,1)S(1)} %get-tuple-element.18, bf16[2,2048,2048]{2,1,0:T(8,128)(2,1)S(1)} %bitcast.49), kind=kOutput, calls=%fused_computation.8 | convolution fusion | flops 1879048192 | bytes 11272192 | tf_op jit(solution)/shard_map/dot_general | solution.py:414
  148.0 109.1 %scatter_sum.1 = (bf16[128,2048]{1,0:T(8,128)(2,1)}, bf16[16,128,224]{2,1,0:T(8,128)(2,1)}) custom-call(bf16[2048,448]{1,0:T(8,128)(2,1)} %pad_maximum_fusion.d_ref, bf16[448,4096]{1,0:T(8,128)(2,1)} %get-tuple-element.9.w_ref, bf16[2048,224]{1,0:T(8,128)(2,1)} %get-tuple-element.16.h_ref), custom_call_target="tpu_custom_call" | custom-call | tf_op jit(solution)/shard_map/scatter_sum/pallas_call | solution.py:351
  257.1 1.6 copy.25
  258.7 1.3 copy.26
  260.0 0.0 copy-start.1
  260.0 6.5 %maximum_multiply_fusion = (f32[224,4096]{1,0:T(8,128)}, f32[224,4096]{1,0:T(8,128)}) fusion(f32[224,2048]{1,0:T(8,128)S(1)} %fusion.2, f32[224,2048]{1,0:T(8,128)} %fusion.10, f32[224,2048]{1,0:T(8,128)} %fusion, f32[224,2048]{1,0:T(8,128)} %fusion.8), kind=kLoop, calls=%fused_computation.24 | loop fusion | flops 3670016 | bytes 14680064 | tf_op jit(solution)/shard_map/div | solution.py:419
  266.5 0.0 copy-done.1
  266.5 0.8 copy.32
  (2 shorter events, 0.0 us)
Async XLA Ops:
  0.6 9.2 %copy-start.2 = (f32[224,16]{0,1:T(8,128)S(1)}, f32[224,16]{0,1:T(8,128)}, u32[]{:S(2)}) copy-start(f32[224,16]{0,1:T(8,128)} %param.8) | copy-start | bytes 43012
  0.6 9.9 %copy-start.3 = (f32[224,16]{0,1:T(8,128)S(1)}, f32[224,16]{0,1:T(8,128)}, u32[]{:S(2)}) copy-start(f32[224,16]{0,1:T(8,128)} %param.10) | copy-start | bytes 43012
  2.9 112.1 %all-to-all-start = ((bf16[128,16,224]{0,2,1:T(8,128)(2,1)}), bf16[128,16,224]{0,2,1:T(8,128)(2,1)S(1)}, u32[]{:S(2)}, u32[]{:S(2)}) async-start(bf16[128,16,224]{0,2,1:T(8,128)(2,1)} %bitcast), calls=%async_computation | async-start | bytes 1835008 | tf_op jit(solution)/shard_map/all_to_all | solution.py:384
  97.5 6.2 %copy-start = (bf16[448,4096]{1,0:T(8,128)(2,1)S(1)}, bf16[448,4096]{1,0:T(8,128)(2,1)}, u32[]{:S(2)}) copy-start(bf16[448,4096]{1,0:T(8,128)(2,1)} %get-tuple-element.9.w_ref) | copy-start | bytes 11010052
  97.6 13.5 %slice-start = ((s8[16777216]{0:T(1024)(128)(4,1)}), s8[4194304]{0:T(1024)(128)(4,1)S(1)}, s32[]{:S(2)}) async-start(s8[16777216]{0:T(1024)(128)(4,1)} %bitcast.46), calls=%async_computation.1 | async-start | bytes 8388608
  97.6 13.5 %slice-start.1 = ((s8[16777216]{0:T(1024)(128)(4,1)}), s8[4194304]{0:T(1024)(128)(4,1)S(1)}, s32[]{:S(2)}) async-start(s8[16777216]{0:T(1024)(128)(4,1)} %bitcast.46), calls=%async_computation.2 | async-start | bytes 8388608
  103.8 7.3 %slice-start.2 = ((s8[16777216]{0:T(1024)(128)(4,1)}), s8[4194304]{0:T(1024)(128)(4,1)S(1)}, s32[]{:S(2)}) async-start(s8[16777216]{0:T(1024)(128)(4,1)} %bitcast.46), calls=%async_computation.3 | async-start | bytes 8388608
  103.8 7.3 %slice-start.3 = ((s8[16777216]{0:T(1024)(128)(4,1)}), s8[4194304]{0:T(1024)(128)(4,1)S(1)}, s32[]{:S(2)}) async-start(s8[16777216]{0:T(1024)(128)(4,1)} %bitcast.46), calls=%async_computation.4 | async-start | bytes 8388608
  126.7 14.6 %slice-start.4 = ((s8[16777216]{0:T(1024)(128)(4,1)}), s8[4194304]{0:T(1024)(128)(4,1)S(1)}, s32[]{:S(2)}) async-start(s8[16777216]{0:T(1024)(128)(4,1)} %bitcast.48), calls=%async_computation.5 | async-start | bytes 8388608
  126.7 14.6 %slice-start.5 = ((s8[16777216]{0:T(1024)(128)(4,1)}), s8[4194304]{0:T(1024)(128)(4,1)S(1)}, s32[]{:S(2)}) async-start(s8[16777216]{0:T(1024)(128)(4,1)} %bitcast.48), calls=%async_computation.6 | async-start | bytes 8388608
  132.3 9.0 %slice-start.6 = ((s8[16777216]{0:T(1024)(128)(4,1)}), s8[4194304]{0:T(1024)(128)(4,1)S(1)}, s32[]{:S(2)}) async-start(s8[16777216]{0:T(1024)(128)(4,1)} %bitcast.48), calls=%async_computation.7 | async-start | bytes 8388608
  132.3 9.0 %slice-start.7 = ((s8[16777216]{0:T(1024)(128)(4,1)}), s8[4194304]{0:T(1024)(128)(4,1)S(1)}, s32[]{:S(2)}) async-start(s8[16777216]{0:T(1024)(128)(4,1)} %bitcast.48), calls=%async_computation.8 | async-start | bytes 8388608
  260.0 6.5 %copy-start.1 = (bf16[128,2048]{1,0:T(8,128)(2,1)S(1)}, bf16[128,2048]{1,0:T(8,128)(2,1)}, u32[]{:S(2)}) copy-start(bf16[128,2048]{1,0:T(8,128)(2,1)} %get-tuple-element.26) | copy-start | bytes 1572868

commit v5 on v4

--- a/solution.py
+++ b/solution.py
@@ -46,13 +46,16 @@
 def gather_kernel(groups, cores, x_ref, gc_ref, gs_ref, uc_ref, us_ref, out_ref, w_ref, own_sem, *sems):
     me, core, z, line = place(groups)
     a, b, sa, sb = bits(me, core % 2)
-    rows = x_ref.shape[0]
+    rows, wide = x_ref.shape
     to_a, to_b, to_z, to_core = peers_of(me, core, z, line, cores, a, b, sa, sb)
     greet([to_a, to_b] + to_z + to_core)
     up_send, down_send, z_recv, b_send, b_recv, a_send, a_recv, c_send, c_recv = sems
 
     def at(slab, block):
-        return out_ref.at[slab, pl.ds(pl.multiple_of(block * rows, rows), rows), :]
+        return out_ref.at[
+            pl.ds(pl.multiple_of(block * rows, rows), rows),
+            pl.ds(pl.multiple_of(slab * wide, wide), wide),
+        ]
 
     def copy_of(src, slab, block, send_sem, recv_sem, peer):
         return pltpu.make_async_remote_copy(
@@ -182,7 +185,7 @@
     return pl.pallas_call(
         functools.partial(gather_kernel, groups, cores),
         out_shape=(
-            jax.ShapeDtypeStruct((cores, groups * rows, wide), tokens.dtype),
+            jax.ShapeDtypeStruct((groups * rows, cores * wide), tokens.dtype),
             jax.ShapeDtypeStruct((2 * gate_codes.shape[0], gate_codes.shape[1]), jnp.bfloat16),
         ),
         in_specs=[pl.BlockSpec(memory_space=pl.ANY)] + [pl.BlockSpec(memory_space=pltpu.VMEM)] * 4,
@@ -380,21 +383,13 @@
     whole, w_both = gather_tokens(
         tokens, gate_codes, gate_scales, up_codes, up_scales, groups, lax.axis_size("intra")
     )
-    slabs, count, wide = whole.shape
     back = lax.all_to_all(cotangent, "inter", split_axis=1, concat_axis=0, tiled=True)
     owned = gate_codes.shape[0]
 
     def forward(weights):
-        total = None
-        for s in range(slabs):
-            term = lax.dot_general(
-                whole[s],
-                weights[:, s * wide:(s + 1) * wide],
-                (((1,), (1,)), ((), ())),
-                preferred_element_type=jnp.float32,
-            )
-            total = term if total is None else total + term
-        return total
+        return lax.dot_general(
+            whole, weights, (((1,), (1,)), ((), ())), preferred_element_type=jnp.float32
+        )
 
     gate = forward(w_both[:owned])
     up = forward(w_both[owned:])
@@ -410,13 +405,9 @@
     hidden = parts.transpose(1, 0, 2).reshape(parts.shape[1], groups * owned)
 
     def rows_grad(d_rows):
-        terms = [
-            lax.dot_general(
-                d_rows, whole[s], (((0,), (0,)), ((), ())), preferred_element_type=jnp.float32
-            )
-            for s in range(slabs)
-        ]
-        return jnp.concatenate(terms, axis=1) / groups
+        return lax.dot_general(
+            d_rows, whole, (((0,), (0,)), ((), ())), preferred_element_type=jnp.float32
+        ) / groups
 
     return (hidden, token_grad, rows_grad(d_gate), rows_grad(d_up))
 

time: 270 us -> 262 us (0.970)
  other arithmetic: 8.81 us -> 2.35 us
    div x1 -> x0, other arithmetic: 6.5 us -> none  [rows_grad(): return jnp.concatenate(terms, axis=1) / groups]
    dot_general x8 -> x4, matrix products: 46.2 us -> 44.8 us  [the longest x2 26.6 us: forward(): lax.dot_general(whole, weights, (((1,), (1,)), ((), ())), preferred_eleme...]
    unnamed x29 -> x19, local copies, waits for them, and re-layouts: 5.83 us -> 5.81 us
  transfers between devices with their start and end apart: 1 -> 1, of which waited for: 0 -> 0; matrix products, arithmetic and copies ran while one was open for 7% -> 5% of each run, Pallas kernels for 32% -> 33%
where the time goes in v5:
time: 262 us; the launch traced here: 260 us
  Pallas kernels  196 us (75%)
  matrix products  44.8 us (17%)
  local copies, waits for them, and re-layouts  9.25 us (4%)
  starting transfers between devices  6.94 us (3%)
    pallas_call x1, Pallas kernels, scatter_sum(): pl.pallas_call(functools.partial(scatter_kernel, groups, cores), out_shap...  109 us
    pallas_call x1, Pallas kernels, gather_tokens(): pl.pallas_call(functools.partial(gather_kernel, groups, cores), out_shape...  86.3 us
    dot_general x2, matrix products, forward(): lax.dot_general(whole, weights, (((1,), (1,)), ((), ())), preferred_eleme...  26.6 us
    dot_general x2, matrix products, rows_grad(): lax.dot_general(d_rows, whole, (((0,), (0,)), ((), ())), preferred_elemen...  18.2 us
    all_to_all x1, starting transfers between devices, per_device(): lax.all_to_all(cotangent, 'inter', split_axis=1, concat_axis=0, tiled=True)  6.94 us
    unnamed x19, local copies, waits for them, and re-layouts  5.81 us
  transfers between devices with their start and end apart: 1, of which 0 were waited for; matrix products, arithmetic and copies ran while one was open for 5% of the time, Pallas kernels for 33%

profile of v5, /device:TPU:28, one launch (start us, length us, event | category | flops | bytes accessed | tf_op | source)
XLA Modules:
  0.0 259.6 jit_solution(7220431193103813628)
XLA Ops:
  0.6 0.0 copy-start.1
  0.6 0.0 copy-start.2
  0.7 2.2 copy.18
  2.9 6.9 %all-to-all-start = ((bf16[128,16,224]{0,2,1:T(8,128)(2,1)}), bf16[128,16,224]{0,2,1:T(8,128)(2,1)S(1)}, u32[]{:S(2)}, u32[]{:S(2)}) async-start(bf16[128,16,224]{0,2,1:T(8,128)(2,1)} %bitcast), calls=%async_computation | async-start | bytes 1835008 | tf_op jit(solution)/shard_map/all_to_all | solution.py:386
  9.8 0.0 copy-done.1
  9.8 0.7 copy.20.gs_ref
  10.6 0.0 copy-done.2
  10.6 0.7 copy.21.us_ref
  11.3 86.3 %gather_tokens.1 = (bf16[2048,4096]{1,0:T(8,128)(2,1)}, bf16[448,4096]{1,0:T(8,128)(2,1)}) custom-call(bf16[128,2048]{1,0:T(8,128)(2,1)} %x_ref.1, bf16[224,4096]{1,0:T(8,128)(2,1)} %gc_ref.1, f32[224,16]{1,0:T(8,128)} %copy.20.gs_ref, bf16[224,4096]{1,0:T(8,128)(2,1)} %uc_ref.1, f32[224,16]{1,0:T(8,128)} %copy.21.us_ref), custom_call_target="tpu_custom_call" | custom-call | tf_op jit(solution)/shard_map/gather_tokens/pallas_call | solution.py:185
  97.6 12.4 %fusion.5 = f32[2048,224]{1,0:T(8,128)} fusion(bf16[2048,4096]{1,0:T(8,128)(2,1)} %get-tuple-element.8, bf16[448,4096]{1,0:T(8,128)(2,1)} %get-tuple-element.9.w_ref), kind=kOutput, calls=%fused_computation.13 | convolution fusion | flops 3758096384 | bytes 20447232 | tf_op jit(solution)/shard_map/dot_general | solution.py:390
  109.9 0.0 all-to-all-done
  109.9 0.2 convert_bitcast_fusion
  110.1 1.8 copy.19
  111.9 0.0 slice-start
  111.9 0.0 slice-start.1
  111.9 0.0 slice-start.2
  111.9 14.2 %multiply_convert_fusion = (bf16[2048,224]{1,0:T(8,128)(2,1)}, bf16[2048,224]{1,0:T(8,128)(2,1)S(1)}, bf16[2048,224]{1,0:T(8,128)(2,1)S(1)}) fusion(f32[2048,224]{1,0:T(8,128)} %fusion.5, f32[16,128,224]{2,1,0:T(8,128)} %copy.19, bf16[2048,4096]{1,0:T(8,128)(2,1)} %get-tuple-element.8, bf16[448,4096]{1,0:T(8,128)(2,1)} %get-tuple-element.9.w_ref), kind=kOutput, calls=%fused_computation.9 | convolution fusion | flops 3764977664 | bytes 25559040 | tf_op jit(solution)/shard_map/dot_general | solution.py:390
  126.1 0.0 slice-start.3
  126.1 11.8 %convolution_multiply_fusion.1 = f32[224,4096]{1,0:T(8,128)} fusion(bf16[2048,224]{1,0:T(8,128)(2,1)S(1)} %get-tuple-element.17, bf16[2048,4096]{1,0:T(8,128)(2,1)} %get-tuple-element.8), kind=kOutput, calls=%fused_computation.1 | convolution fusion | flops 3759013888 | bytes 21364736 | tf_op jit(solution)/shard_map/dot_general | solution.py:408
  138.0 2.2 pad_maximum_fusion.d_ref
  140.1 0.0 slice-done
  140.1 0.0 slice-done.1
  140.1 0.0 slice-done.2
  140.1 0.0 slice-done.3
  140.2 6.4 %convolution_multiply_fusion = f32[224,4096]{1,0:T(8,128)} fusion(bf16[2048,224]{1,0:T(8,128)(2,1)S(1)} %get-tuple-element.18, bf16[2048,4096]{1,0:T(8,128)(2,1)S(1)} %bitcast.23), kind=kOutput, calls=%fused_computation | convolution fusion | flops 3759013888 | bytes 21364736 | tf_op jit(solution)/shard_map/dot_general | solution.py:408
  146.5 109.4 %scatter_sum.1 = (bf16[128,2048]{1,0:T(8,128)(2,1)}, bf16[16,128,224]{2,1,0:T(8,128)(2,1)}) custom-call(bf16[2048,448]{1,0:T(8,128)(2,1)} %pad_maximum_fusion.d_ref, bf16[448,4096]{1,0:T(8,128)(2,1)} %get-tuple-element.9.w_ref, bf16[2048,224]{1,0:T(8,128)(2,1)} %get-tuple-element.16.h_ref), custom_call_target="tpu_custom_call" | custom-call | tf_op jit(solution)/shard_map/scatter_sum/pallas_call | solution.py:354
  255.9 0.0 copy-start
  255.9 1.6 copy.27
  257.6 1.3 copy.28
  258.8 0.0 copy-done
  258.8 0.8 copy.32
  (1 shorter events, 0.0 us)
Async XLA Ops:
  0.6 9.2 %copy-start.1 = (f32[224,16]{0,1:T(8,128)S(1)}, f32[224,16]{0,1:T(8,128)}, u32[]{:S(2)}) copy-start(f32[224,16]{0,1:T(8,128)} %param.8) | copy-start | bytes 43012
  0.6 9.9 %copy-start.2 = (f32[224,16]{0,1:T(8,128)S(1)}, f32[224,16]{0,1:T(8,128)}, u32[]{:S(2)}) copy-start(f32[224,16]{0,1:T(8,128)} %param.10) | copy-start | bytes 43012
  2.9 107.1 %all-to-all-start = ((bf16[128,16,224]{0,2,1:T(8,128)(2,1)}), bf16[128,16,224]{0,2,1:T(8,128)(2,1)S(1)}, u32[]{:S(2)}, u32[]{:S(2)}) async-start(bf16[128,16,224]{0,2,1:T(8,128)(2,1)} %bitcast), calls=%async_computation | async-start | bytes 1835008 | tf_op jit(solution)/shard_map/all_to_all | solution.py:386
  111.9 28.2 %slice-start = ((s8[16777216]{0:T(1024)(128)(4,1)}), s8[4194304]{0:T(1024)(128)(4,1)S(1)}, s32[]{:S(2)}) async-start(s8[16777216]{0:T(1024)(128)(4,1)} %bitcast.22), calls=%async_computation.1 | async-start | bytes 8388608
  111.9 28.2 %slice-start.1 = ((s8[16777216]{0:T(1024)(128)(4,1)}), s8[4194304]{0:T(1024)(128)(4,1)S(1)}, s32[]{:S(2)}) async-start(s8[16777216]{0:T(1024)(128)(4,1)} %bitcast.22), calls=%async_computation.2 | async-start | bytes 8388608
  111.9 28.2 %slice-start.2 = ((s8[16777216]{0:T(1024)(128)(4,1)}), s8[4194304]{0:T(1024)(128)(4,1)S(1)}, s32[]{:S(2)}) async-start(s8[16777216]{0:T(1024)(128)(4,1)} %bitcast.22), calls=%async_computation.3 | async-start | bytes 8388608
  126.1 14.0 %slice-start.3 = ((s8[16777216]{0:T(1024)(128)(4,1)}), s8[4194304]{0:T(1024)(128)(4,1)S(1)}, s32[]{:S(2)}) async-start(s8[16777216]{0:T(1024)(128)(4,1)} %bitcast.22), calls=%async_computation.4 | async-start | bytes 8388608
  255.9 2.9 %copy-start = (bf16[128,2048]{1,0:T(8,128)(2,1)S(1)}, bf16[128,2048]{1,0:T(8,128)(2,1)}, u32[]{:S(2)}) copy-start(bf16[128,2048]{1,0:T(8,128)(2,1)} %get-tuple-element.24) | copy-start | bytes 1572868
